TPU v7x, 32 devices: a whole 2x2x4 slice. The times are simulated.
32 devices in a mesh: groups: 2 (over y), wide: 8 (over z, x), short: 2 (over core).
Axes of the slice: x: 2, y: 2, z: 4, core: 2. Of those that a mesh axis runs over, the one named last changes fastest.
Arguments:
- tokens: bfloat16 [64, 5120], P(('groups', 'wide'), 'short'), parts along dimension 0, may hold values from -6 to 6
- norm_gain: float32 [5120], P('short'), may hold values from 0.5 to 1.5
- mixer_in: bfloat16 [5120, 2, 5888], P('short', None, 'wide'), may hold values from -0.078125 to 0.078125
- shared_in: bfloat16 [5120, 512], P('short', 'wide'), may hold values from -0.078125 to 0.078125
- step_in: bfloat16 [5120, 32], P('short'), may hold values from -0.078125 to 0.078125
- step_bias: float32 [32], P('short'), may hold values from -2 to 1
- decay_rate: float32 [32], P('short'), may hold values from 0.05 to 4
- skip_gain: float32 [32], P('short'), may hold values from 0.2 to 1.5
- cached_keys: bfloat16 [16, 512, 512], P(('groups', 'wide'), None, 'short'), parts along dimension 0, may hold values from -64 to 64
- cached_values: bfloat16 [16, 512, 512], P(('groups', 'wide'), None, 'short'), parts along dimension 0, may hold values from -6 to 6
- lengths: int32 [16], P(('groups', 'wide')), parts along dimension 0, may hold values from 2 to 512, as said below
- state_cache: bfloat16 [16, 32, 128, 256], P(('groups', 'wide'), 'short'), parts along dimension 0, may hold values from -6 to 6
- mixer_gain: float32 [4096], P('short'), may hold values from 0.5 to 1.5
- mixer_out: bfloat16 [2, 3328, 5120], P(None, 'wide', 'short'), may hold values from -0.078125 to 0.078125
- gate_weight: bfloat16 [5120, 21504], P('short', 'wide'), may hold values from -0.078125 to 0.078125
- up_weight: bfloat16 [5120, 21504], P('short', 'wide'), may hold values from -0.078125 to 0.078125
- down_weight: bfloat16 [21504, 5120], P('wide', 'short'), may hold values from -0.0390625 to 0.0390625
Outputs:
- mixed: bfloat16 [64, 5120], P(('groups', 'wide'), 'short'), parts along dimension 0
There are 2 independent parts, one for each index of `groups`. A program takes and returns all parts, laid end to end along the dimension named above; an argument that names none is the same for every part. Nothing has to cross between parts.
Inputs may be any that keep to these rules, and one draw needn't show every extreme that they name: `lengths`: in every draw some request holds exactly 512 earlier tokens.
All inputs are finite; a program needn't handle non-finite values.
Results may differ from a plain program's by a relative error of at most 0.009.
Values may be sent and summed in bfloat16 or wider, within the bound.
A program may use at most 128 MiB of HBM per device.

v0:
```python
import functools
import jax
import jax.numpy as jnp
from jax import lax
from jax.experimental import pallas as pl
from jax.experimental.pallas import tpu as pltpu
from jax.sharding import PartitionSpec as P

D = 5120
QUERY_HEADS = 20
KEY_VALUE_HEADS = 4
HEAD_SIZE = 128
MH = 32
MP = 128
NS = 256
CACHE_SLOTS = 512
DRAFT_TOKENS = 4


epsilon = 1e-05


def as_sent(x):

    def short(part):
        return part.astype(jnp.bfloat16) if part.dtype == jnp.float32 else part

    return jax.tree.map(short, x)


def rotate(vectors, cos_table, sin_table):
    half_width = vectors.shape[-1] // 2
    first_half = vectors[..., :half_width]
    second_half = vectors[..., half_width:]
    return jnp.concatenate(
        [
            first_half * cos_table - second_half * sin_table,
            second_half * cos_table + first_half * sin_table,
        ],
        axis=-1,
    )


def rope_tables(positions):
    frequency = 10000.0 ** (-(jnp.arange(HEAD_SIZE // 2, dtype=jnp.float32) * 2.0 / HEAD_SIZE))
    angles = positions.astype(jnp.float32)[..., None] * frequency
    return (jnp.cos(angles), jnp.sin(angles))


def attend_one(queries, fresh_keys, fresh_values, key_tile_block, value_tile_block, length):
    score_scale = HEAD_SIZE ** (-0.5)
    scores_cache = (
        jnp.einsum("tkgd,pkd->kgtp", queries, key_tile_block, preferred_element_type=jnp.float32)
        * score_scale
    )
    scores_new = (
        jnp.einsum("tkgd,ukd->kgtu", queries, fresh_keys, preferred_element_type=jnp.float32)
        * score_scale
    )
    live_keys = jnp.arange(key_tile_block.shape[0], dtype=jnp.int32) < length
    causal = jnp.arange(DRAFT_TOKENS)[None, :] <= jnp.arange(DRAFT_TOKENS)[:, None]
    scores_cache = jnp.where(live_keys, scores_cache, -1e30)
    scores_new = jnp.where(causal, scores_new, -1e30)
    highest = jnp.maximum(jnp.max(scores_cache, axis=-1), jnp.max(scores_new, axis=-1))[..., None]
    weight_cache = jnp.exp(scores_cache - highest)
    weight_new = jnp.exp(scores_new - highest)
    denominator = jnp.sum(weight_cache, axis=-1, keepdims=True) + jnp.sum(
        weight_new, axis=-1, keepdims=True
    )
    probs_cache = (weight_cache / denominator).astype(jnp.bfloat16)
    probs_new = (weight_new / denominator).astype(jnp.bfloat16)
    attended = jnp.einsum(
        "kgtp,pkd->tkgd", probs_cache, value_tile_block, preferred_element_type=jnp.float32
    )
    attended = attended + jnp.einsum(
        "kgtu,ukd->tkgd", probs_new, fresh_values, preferred_element_type=jnp.float32
    )
    return attended.astype(jnp.bfloat16)


def scan_one(
    state_block, inputs_x, gates_z, b_vals, c_vals, step_sizes, decay_rates, skip_gain, head_gain
):
    hstate = state_block.astype(jnp.float32)
    in_active = jax.nn.silu(inputs_x.astype(jnp.float32))
    write_vec = jax.nn.silu(b_vals.astype(jnp.float32))
    read_vec = jax.nn.silu(c_vals.astype(jnp.float32))
    outputs = []
    for draft_index in range(DRAFT_TOKENS):
        decays = jnp.exp(-step_sizes[draft_index] * decay_rates)
        inject = (step_sizes[draft_index][:, None] * in_active[draft_index])[
            :, :, None
        ] * write_vec[draft_index][None, None, :]
        hstate = decays[:, None, None] * hstate + inject
        readout = jnp.einsum(
            "hpn,n->hp", hstate, read_vec[draft_index], precision=lax.Precision.HIGHEST
        )
        outputs.append(readout + skip_gain[:, None] * in_active[draft_index])
    gated = jnp.stack(outputs) * jax.nn.silu(gates_z.astype(jnp.float32))
    mean_square = jnp.mean(gated * gated, axis=-1, keepdims=True)
    return (gated * lax.rsqrt(mean_square + epsilon) * head_gain).astype(jnp.bfloat16)


def on_device(
    tokens,
    norm_gain,
    mixer_in,
    shared_in,
    step_in,
    step_bias,
    decay_rate,
    skip_gain,
    cached_keys,
    cached_values,
    lengths,
    state_cache,
    mixer_gain,
    mixer_out,
    gate_weight,
    up_weight,
    down_weight,
):
    short_count = lax.axis_size("short")
    n_wide = lax.axis_size("wide")
    q_heads = QUERY_HEADS // short_count
    key_value_heads = KEY_VALUE_HEADS // short_count
    ssm_heads = MH // short_count
    repeat_factor = QUERY_HEADS // KEY_VALUE_HEADS
    query_size = q_heads * HEAD_SIZE
    key_size = key_value_heads * HEAD_SIZE
    m_size = ssm_heads * MP
    local_rows = tokens.shape[0]
    requests = local_rows // DRAFT_TOKENS
    width_half = tokens.shape[1]
    rows_float = tokens.astype(jnp.float32)
    square_sum = lax.psum(jnp.sum(rows_float * rows_float, axis=1), "short")
    inv_rms = lax.rsqrt(square_sum / D + epsilon)
    normed = (rows_float * inv_rms[:, None] * norm_gain[None, :]).astype(jnp.bfloat16)
    step_terms = jnp.dot(normed, step_in, preferred_element_type=jnp.float32)
    step_raw = lax.psum_scatter(step_terms, "short", scatter_dimension=1, tiled=True)
    gathered = lax.all_gather(normed, "wide", axis=0, tiled=True)
    group_part = jnp.einsum("rd,dgc->rgc", gathered, mixer_in, preferred_element_type=jnp.float32)
    shared_part = jnp.dot(gathered, shared_in, preferred_element_type=jnp.float32)[:, None, :]
    gate_part = jnp.dot(gathered, gate_weight, preferred_element_type=jnp.float32)
    up_part = jnp.dot(gathered, up_weight, preferred_element_type=jnp.float32)
    gate_half, up_half = (
        lax.psum_scatter(
            gate_part.astype(jnp.bfloat16), "short", scatter_dimension=0, tiled=True
        ).astype(jnp.float32),
        lax.psum_scatter(
            up_part.astype(jnp.bfloat16), "short", scatter_dimension=0, tiled=True
        ).astype(jnp.float32),
    )
    hidden_half = (jax.nn.silu(gate_half) * up_half).astype(jnp.bfloat16)
    hidden = lax.all_gather(hidden_half, "short", axis=0, tiled=True)
    group_moved, shared_moved = (
        lax.all_to_all(group_part, "wide", split_axis=0, concat_axis=2, tiled=True),
        lax.all_to_all(shared_part, "wide", split_axis=0, concat_axis=2, tiled=True),
    )
    group_sum = lax.psum_scatter(group_moved, "short", scatter_dimension=1, tiled=True)
    shared_sum = lax.psum(shared_moved, "short")
    features = group_sum[:, 0, :].astype(jnp.bfloat16)
    shared_vals = shared_sum[:, 0, :].astype(jnp.bfloat16)
    queries = features[:, :query_size].reshape(requests, DRAFT_TOKENS, q_heads, HEAD_SIZE)
    fresh_keys = features[:, query_size : query_size + key_size].reshape(
        requests, DRAFT_TOKENS, key_value_heads, HEAD_SIZE
    )
    fresh_values = features[:, query_size + key_size : query_size + 2 * key_size].reshape(
        requests, DRAFT_TOKENS, key_value_heads, HEAD_SIZE
    )
    x_start = query_size + 2 * key_size
    inputs_x = features[:, x_start : x_start + m_size].reshape(
        requests, DRAFT_TOKENS, ssm_heads, MP
    )
    gates_z = features[:, x_start + m_size : x_start + 2 * m_size].reshape(
        requests, DRAFT_TOKENS, ssm_heads, MP
    )
    positions = lengths[:, None] + jnp.arange(DRAFT_TOKENS, dtype=jnp.int32)[None, :]
    cos_table, sin_table = rope_tables(positions)
    cos_table = cos_table[:, :, None, :]
    sin_table = sin_table[:, :, None, :]
    rotated_queries = rotate(queries.astype(jnp.float32), cos_table, sin_table).astype(jnp.bfloat16)
    keys_rot = rotate(fresh_keys.astype(jnp.float32), cos_table, sin_table).astype(jnp.bfloat16)
    rotated_queries = rotated_queries.reshape(
        requests, DRAFT_TOKENS, key_value_heads, repeat_factor, HEAD_SIZE
    )
    key_tile_block = cached_keys.reshape(requests, CACHE_SLOTS, key_value_heads, HEAD_SIZE)
    value_tile_block = cached_values.reshape(requests, CACHE_SLOTS, key_value_heads, HEAD_SIZE)
    attention = jax.vmap(attend_one)(
        rotated_queries, keys_rot, fresh_values, key_tile_block, value_tile_block, lengths
    )
    step_sizes = jax.nn.softplus(
        step_raw.reshape(requests, DRAFT_TOKENS, ssm_heads) + step_bias[None, None, :]
    )
    b_vals = shared_vals[:, :NS].reshape(requests, DRAFT_TOKENS, NS)
    c_vals = shared_vals[:, NS:].reshape(requests, DRAFT_TOKENS, NS)
    head_gain = mixer_gain.reshape(ssm_heads, MP)
    mamba = jax.vmap(scan_one, in_axes=(0, 0, 0, 0, 0, 0, None, None, None))(
        state_cache, inputs_x, gates_z, b_vals, c_vals, step_sizes, decay_rate, skip_gain, head_gain
    )
    own_rows = jnp.concatenate(
        [attention.reshape(local_rows, query_size), mamba.reshape(local_rows, m_size)], axis=1
    )
    returned = lax.all_to_all(
        as_sent(own_rows[:, None, :]), "wide", split_axis=2, concat_axis=0, tiled=True
    )
    both_groups = lax.all_gather(as_sent(returned), "short", axis=1, tiled=True).astype(
        returned.dtype
    )
    projected = jnp.einsum(
        "rgc,gcd->rd", both_groups, mixer_out, preferred_element_type=jnp.float32
    )
    summed = projected + jnp.dot(hidden, down_weight, preferred_element_type=jnp.float32)
    pieces = lax.all_to_all(
        summed.reshape(n_wide, local_rows, width_half).astype(jnp.bfloat16),
        "wide",
        split_axis=0,
        concat_axis=0,
        tiled=True,
    ).astype(jnp.float32)
    total = rows_float + jnp.sum(pieces, axis=0)
    return total.astype(jnp.bfloat16)


MESH = pl.DeviceIdType.MESH
F32 = jnp.float32
BF16 = jnp.bfloat16
NT = (((1,), (1,)), ((), ()))
LANE = 128


def silu(v):
    return v / (1.0 + jnp.exp(-v))


def dot(a, b):
    return jnp.dot(a, b, preferred_element_type=F32)


def dot_nt(a, b):
    return lax.dot_general(a, b, NT, preferred_element_type=F32)


def fused_kernel(
    dims,
    tokens, gain, bias, rate, skip, lengths, cosf, sinf, mixer_gain,
    mixer_in, shared_in, step_in, keys, values, state, mixer_out, gate, up, down,
    out,
    w_a, w_b, k_v, v_v, s_v, g_v, u_v, m_v, d_v,
    xg, xf, xb, sq_send, sq_recv, p_send, p_recv, c_b, tot, step_f,
    f_send, f_recv, feat, bc, qbuf, knbuf, vnbuf, obuf, cbuf, rbuf, own,
    m_send, m_recv, lhs, gsc, gu_send, gu_recv, hbuf, o_send, o_recv,
    sem_w, sem_loc, sem_gs, sem_gr, sem_ps, sem_pr, sem_fs, sem_fr,
    sem_ms, sem_mr, sem_us, sem_ur, sem_hs, sem_hr, sem_os, sem_or,
):
    n, n_short, rows, width, gcol, scol, ncol, ocol, n_chunk, fchunk, n_oc, ochunk = dims
    total_rows = n * rows
    me = lax.axis_index("wide")
    s = lax.axis_index("short")
    other = 1 - s
    q_heads = QUERY_HEADS // n_short
    kv_heads = KEY_VALUE_HEADS // n_short
    m_heads = MH // n_short
    rep = QUERY_HEADS // KEY_VALUE_HEADS
    acol = gcol + scol + ncol
    fpad = xpad(gcol)
    opad = round_up(ocol)

    def peer(d):
        return lax.rem(me + d, n)

    weights = []

    def fetch(src, dst):
        copy = pltpu.make_async_copy(src, dst, sem_w.at[len(weights)])
        copy.start()
        weights.append(copy)
        return copy

    fa = [
        fetch(mixer_in.at[other], w_a.at[pl.ds(0, gcol)]),
        fetch(shared_in, w_a.at[pl.ds(gcol, scol)]),
        fetch(step_in, w_a.at[pl.ds(gcol + scol, ncol)]),
    ]
    fb = [fetch(mixer_in.at[s], w_b)]

    barrier = pltpu.get_barrier_semaphore()
    for d in range(n):
        for e in range(n_short):
            if d or e:
                pl.semaphore_signal(
                    barrier, inc=1,
                    device_id={"wide": peer(d), "short": lax.rem(s + e, n_short)},
                    device_id_type=MESH,
                )

    def cols(c):
        return pl.ds(c * fchunk, fchunk)

    fgu = []
    for c in range(n_chunk):
        fgu.append((fetch(gate.at[:, cols(c)], g_v.at[c]), fetch(up.at[:, cols(c)], u_v.at[c])))
        if c == 0:
            fkv = [fetch(keys, k_v), fetch(values, v_v), fetch(state, s_v)]
    fmo = [fetch(mixer_out.at[g], m_v.at[g, pl.ds(0, ocol)]) for g in range(n_short)]
    fdn = [fetch(down.at[:, pl.ds(o * ochunk, ochunk)], d_v.at[o]) for o in range(n_oc)]

    pl.semaphore_wait(barrier, n * n_short - 1)

    def remote(src, dst, send, recv, wide, short):
        copy = pltpu.make_async_remote_copy(
            src_ref=src, dst_ref=dst, send_sem=send, recv_sem=recv,
            device_id={"wide": wide, "short": short}, device_id_type=MESH,
        )
        copy.start()
        return copy

    def arrived(buf, recv):
        pltpu.make_async_copy(buf, buf, recv).wait()

    sent = []

    for d in range(1, n):
        sent.append(remote(tokens, xg.at[me], sem_gs.at[d], sem_gr.at[me], peer(d), s))
    own_tokens = pltpu.make_async_copy(tokens, xg.at[me], sem_loc.at[0])
    own_tokens.start()
    for g in range(n_short):
        if opad > ocol:
            m_v[g, ocol:opad, :] = jnp.zeros((opad - ocol, width), BF16)
    feat[...] = jnp.zeros_like(feat)
    bc[...] = jnp.zeros_like(bc)
    qbuf[...] = jnp.zeros_like(qbuf)
    knbuf[...] = jnp.zeros_like(knbuf)
    vnbuf[...] = jnp.zeros_like(vnbuf)
    cbuf[...] = jnp.zeros_like(cbuf)
    c_b[...] = jnp.zeros_like(c_b)
    tot[...] = jnp.zeros_like(tot)
    own[...] = jnp.zeros_like(own)
    own_tokens.wait()
    for d in range(1, n):
        arrived(xg.at[peer(d)], sem_gr.at[peer(d)])
    for j in range(n):
        xf[rows * j : rows * (j + 1), :] = xg[j].astype(F32)
    x = xf[...]
    sq_send[...] = jnp.broadcast_to(jnp.sum(x * x, axis=1, keepdims=True), sq_send.shape)
    sent.append(remote(sq_send, sq_recv, sem_ps.at[0], sem_pr.at[0], me, other))
    xb[...] = (x * gain[...]).astype(BF16)

    for copy in fa:
        copy.wait()
    p_send[...] = dot_nt(xb[...], w_a[...])
    sent.append(remote(p_send, p_recv, sem_ps.at[1], sem_pr.at[1], me, other))
    fb[0].wait()
    c_b[:, :gcol] = dot_nt(xb[...], w_b[...])
    lane = lax.broadcasted_iota(jnp.int32, (total_rows, acol), 1)
    mine = jnp.where(lane < gcol, c_b[:, :acol], p_send[...])
    arrived(sq_recv, sem_pr.at[0])
    mean_square = (sq_send[:, :1] + sq_recv[:, :1]) / D
    inv = lax.rsqrt(mean_square + epsilon)
    arrived(p_recv, sem_pr.at[1])
    tot[:, :acol] = (mine + p_recv[...]) * inv
    whole = tot[...]
    wide_lane = lax.broadcasted_iota(jnp.int32, whole.shape, 1)
    span = whole.shape[1]
    features = pltpu.roll(
        jnp.where(wide_lane < gcol, whole, 0.0), lax.rem(me * gcol, LANE), 1
    )
    low = pltpu.roll(whole, span - gcol, 1)[:, :LANE]
    low_lane = lax.broadcasted_iota(jnp.int32, low.shape, 1)
    low = pltpu.roll(jnp.where(low_lane < scol, low, 0.0), lax.rem(me * scol, LANE), 1)
    step_all = pltpu.roll(whole, span - gcol - scol, 1)[:, :LANE]
    step_f[...] = pltpu.roll(step_all, lax.rem(LANE - s * m_heads, LANE), 1)
    tot[...] = features
    c_b[:, :LANE] = low
    for r in range(n):
        f_send[r, :, :fpad] = tot[rows * r : rows * (r + 1), :].astype(BF16)
        f_send[r, :, fpad:] = c_b[rows * r : rows * (r + 1), :LANE].astype(BF16)
    for d in range(1, n):
        to = peer(d)
        sent.append(remote(f_send.at[to], f_recv.at[me], sem_fs.at[d], sem_fr.at[me], to, s))
    own_f = pltpu.make_async_copy(f_send.at[me], f_recv.at[me], sem_loc.at[1])
    own_f.start()

    half = total_rows // n_short

    def gate_up(c):
        fgu[c][0].wait()
        for i in range(n_short):
            pass
        both = [dot(xb[...], g_v[c])]
        fgu[c][1].wait()
        both.append(dot(xb[...], u_v[c]))
        for k in range(2):
            for i in range(n_short):
                gsc[c, k, i] = both[k][half * i : half * (i + 1)] * inv[half * i : half * (i + 1)]
        for k in range(2):
            gu_send[c, k] = gsc[c, k, other].astype(BF16)
        sent.append(remote(gu_send.at[c], gu_recv.at[c], sem_us.at[c], sem_ur.at[c], me, other))

    def hidden(c):
        arrived(gu_recv.at[c], sem_ur.at[c])
        a = gsc[c, 0, s] + gu_recv[c, 0].astype(F32)
        b = gsc[c, 1, s] + gu_recv[c, 1].astype(F32)
        hbuf[c, s] = (silu(a) * b).astype(BF16)
        sent.append(
            remote(hbuf.at[c, s], hbuf.at[c, s], sem_hs.at[c], sem_hr.at[c], me, other)
        )

    gate_up(0)

    own_f.wait()
    for d in range(1, n):
        arrived(f_recv.at[peer(d)], sem_fr.at[peer(d)])
    fwidth = feat.shape[1]
    for j in range(n):
        base = gcol * j // LANE * LANE
        w = min(fpad, fwidth - base)
        feat[:, base : base + w] += f_recv[j, :, :w].astype(F32)
        base = scol * j // LANE * LANE
        bc[:, base : base + LANE] += f_recv[j, :, fpad:].astype(F32)
    for copy in fkv:
        copy.wait()
    k_at = q_heads * HEAD_SIZE
    v_at = k_at + kv_heads * HEAD_SIZE
    x_at = v_at + kv_heads * HEAD_SIZE
    z_at = x_at + m_heads * MP
    cos_t = cosf[...]
    sin_t = sinf[...]

    def turn(v):
        return v * cos_t + jnp.concatenate([v[:, HEAD_SIZE // 2 :], v[:, : HEAD_SIZE // 2]], axis=1) * sin_t

    length = lengths[0]
    for kv in range(kv_heads):
        for i in range(rep):
            h = kv * rep + i
            qbuf[kv, rows * i : rows * (i + 1), :] = turn(feat[:, h * HEAD_SIZE : (h + 1) * HEAD_SIZE])
        knbuf[kv, :rows, :] = turn(feat[:, k_at + kv * HEAD_SIZE : k_at + (kv + 1) * HEAD_SIZE])
        vnbuf[kv, :rows, :] = feat[:, v_at + kv * HEAD_SIZE : v_at + (kv + 1) * HEAD_SIZE]
        head = slice(kv * HEAD_SIZE, (kv + 1) * HEAD_SIZE)
        query = qbuf[kv].astype(BF16)
        scale = HEAD_SIZE ** (-0.5)
        old = dot_nt(query, k_v[:, head]) * scale
        new = dot_nt(query, knbuf[kv].astype(BF16)) * scale
        slot = lax.broadcasted_iota(jnp.int32, old.shape, 1)
        old = jnp.where(slot < length, old, -1e30)
        token = lax.rem(lax.broadcasted_iota(jnp.int32, new.shape, 0), rows)
        fresh = lax.broadcasted_iota(jnp.int32, new.shape, 1)
        new = jnp.where(fresh <= token, new, -1e30)
        top = jnp.maximum(
            jnp.max(old, axis=1, keepdims=True), jnp.max(new, axis=1, keepdims=True)
        )
        old = jnp.exp(old - top)
        new = jnp.exp(new - top)
        den = jnp.sum(old, axis=1, keepdims=True) + jnp.sum(new, axis=1, keepdims=True)
        obuf[kv] = dot((old / den).astype(BF16), v_v[:, head]) + dot(
            (new / den).astype(BF16), vnbuf[kv].astype(BF16)
        )
        for i in range(rep):
            h = kv * rep + i
            own[:, h * HEAD_SIZE : (h + 1) * HEAD_SIZE] = obuf[kv, rows * i : rows * (i + 1), :]

    write = silu(bc[:, :NS])
    read = silu(bc[:, NS:])
    rest = read
    for i in range(3):
        piece = rest.astype(BF16).astype(F32)
        cbuf[rows * i : rows * (i + 1), :] = piece
        rest = rest - piece
    rbuf[...] = dot_nt(cbuf[...].astype(BF16), s_v[...])
    carried = rbuf[:rows] + rbuf[rows : 2 * rows] + rbuf[2 * rows : 3 * rows]
    raw = step_f[pl.ds(rows * me, rows), :][:, :m_heads] + bias[...]
    step = jnp.maximum(raw, 0.0) + jnp.log1p(jnp.exp(-jnp.abs(raw)))
    run = [step[:1]]
    for t in range(1, rows):
        run.append(run[-1] + step[t : t + 1])
    age = jnp.concatenate(run, axis=0) * rate[...]
    kept = jnp.exp(-age)
    tid = lax.broadcasted_iota(jnp.int32, age.shape, 0)
    mix = []
    for u in range(rows):
        overlap = jnp.sum(read * write[u : u + 1], axis=1, keepdims=True)
        fade = jnp.exp(-jnp.maximum(age - age[u : u + 1], 0.0))
        mix.append(jnp.where(tid >= u, fade, 0.0) * step[u : u + 1] * overlap)
    skips = skip[...]
    for h in range(m_heads):
        hs = slice(h * MP, (h + 1) * MP)
        active = silu(feat[:, x_at + h * MP : x_at + (h + 1) * MP])
        y = kept[:, h : h + 1] * carried[:, hs] + skips[:, h : h + 1] * active
        for u in range(rows):
            y = y + mix[u][:, h : h + 1] * active[u : u + 1]
        y = y * silu(feat[:, z_at + h * MP : z_at + (h + 1) * MP])
        ms = jnp.mean(y * y, axis=1, keepdims=True)
        at = (q_heads + h) * MP
        own[:, at : at + MP] = y * lax.rsqrt(ms + epsilon) * mixer_gain[:, hs]

    window = opad + LANE
    for j in range(n):
        base = ocol * j // LANE * LANE
        off = ocol * j - base
        v = own[:, base : base + window]
        if off:
            v = jnp.concatenate([v[:, off:], v[:, :off]], axis=1)
        m_send[j] = v[:, :opad].astype(BF16)
    for d in range(n):
        to = peer(d)
        for e in range(n_short):
            if d or e:
                sent.append(
                    remote(
                        m_send.at[to], m_recv.at[s, me], sem_ms.at[d, e], sem_mr.at[s, me],
                        to, lax.rem(s + e, n_short),
                    )
                )
    own_m = pltpu.make_async_copy(m_send.at[me], m_recv.at[s, me], sem_loc.at[2])
    own_m.start()

    hidden(0)
    for c in range(1, n_chunk):
        gate_up(c)
        if c > 1:
            hidden(c - 1)
    own_m.wait()
    for d in range(n):
        for e in range(n_short):
            if d or e:
                g = lax.rem(s + e, n_short)
                arrived(m_recv.at[g, peer(d)], sem_mr.at[g, peer(d)])
    for g in range(n_short):
        for j in range(n):
            lhs[g, rows * j : rows * (j + 1), :] = m_recv[g, j].astype(F32)
    if n_chunk > 1:
        hidden(n_chunk - 1)
    for copy in fmo:
        copy.wait()
    for c in range(n_chunk):
        arrived(hbuf.at[c, other], sem_hr.at[c])
    for o in range(n_oc):
        oc = slice(o * ochunk, (o + 1) * ochunk)
        acc = dot(lhs[0].astype(BF16), m_v[0, :, oc])
        for g in range(1, n_short):
            acc = acc + dot(lhs[g].astype(BF16), m_v[g, :, oc])
        fdn[o].wait()
        for c in range(n_chunk):
            acc = acc + dot(
                hbuf[c].reshape(total_rows, fchunk), d_v[o, c * fchunk : (c + 1) * fchunk, :]
            )
        xf[:, oc] = acc
        for r in range(n):
            o_send[o, r] = xf[rows * r : rows * (r + 1), oc].astype(BF16)
        for d in range(1, n):
            to = peer(d)
            sent.append(
                remote(
                    o_send.at[o, to], o_recv.at[o, me], sem_os.at[o, d], sem_or.at[o, me], to, s
                )
            )
    for o in range(n_oc):
        oc = slice(o * ochunk, (o + 1) * ochunk)
        acc = tokens[:, oc].astype(F32) + o_send[o, me].astype(F32)
        for d in range(1, n):
            arrived(o_recv.at[o, peer(d)], sem_or.at[o, peer(d)])
            acc = acc + o_recv[o, peer(d)].astype(F32)
        out[:, oc] = acc.astype(BF16)
    for copy in sent:
        copy.wait_send()


def round_up(v):
    return -(-v // LANE) * LANE


def xpad(gcol):
    return round_up(gcol + LANE - 1)


def pieces_of(width, most):
    tiles = width // LANE
    for k in range(most, 0, -1):
        if tiles % k == 0:
            return k
    return 1


def fused(*args):
    (tokens, norm_gain, mixer_in, shared_in, step_in, step_bias, decay_rate, skip_gain,
     cached_keys, cached_values, lengths, state_cache, mixer_gain, mixer_out,
     gate_weight, up_weight, down_weight) = args
    n = lax.axis_size("wide")
    n_short = lax.axis_size("short")
    rows, width = tokens.shape
    gcol = mixer_in.shape[2]
    scol = shared_in.shape[1]
    ncol = step_in.shape[1]
    ocol = mixer_out.shape[1]
    ffl = gate_weight.shape[1]
    n_chunk = pieces_of(ffl, 3)
    fchunk = ffl // n_chunk
    n_oc = pieces_of(width, 4)
    ochunk = width // n_oc
    m_heads = MH // n_short
    kv_heads = KEY_VALUE_HEADS // n_short
    total_rows = n * rows
    acol = gcol + scol + ncol
    fpad = xpad(gcol)
    opad = round_up(ocol)
    features = n * gcol
    outs = n * ocol
    half = total_rows // n_short
    positions = lengths + jnp.arange(rows, dtype=jnp.int32)
    cos_table, sin_table = rope_tables(positions)
    cosf = jnp.concatenate([cos_table, cos_table], axis=-1)
    sinf = jnp.concatenate([-sin_table, sin_table], axis=-1)
    dims = (n, n_short, rows, width, gcol, scol, ncol, ocol, n_chunk, fchunk, n_oc, ochunk)
    vm = pl.BlockSpec(memory_space=pltpu.VMEM)
    sm = pl.BlockSpec(memory_space=pltpu.SMEM)
    hb = pl.BlockSpec(memory_space=pl.ANY)
    V = pltpu.VMEM
    dma = pltpu.SemaphoreType.DMA
    kvw = cached_keys.shape[2]
    slots = cached_keys.shape[1]
    scratch = [
        V((acol, width), BF16), V((gcol, width), BF16), V((slots, kvw), BF16),
        V((slots, kvw), BF16), V((m_heads * MP, NS), BF16),
        V((n_chunk, width, fchunk), BF16), V((n_chunk, width, fchunk), BF16),
        V((n_short, opad, width), BF16), V((n_oc, ffl, ochunk), BF16),
        V((n, rows, width), BF16), V((total_rows, width), F32), V((total_rows, width), BF16),
        V((total_rows, LANE), F32), V((total_rows, LANE), F32),
        V((total_rows, acol), F32), V((total_rows, acol), F32), V((total_rows, fpad), F32),
        V((total_rows, fpad), F32), V((total_rows, LANE), F32),
        V((n, rows, fpad + LANE), BF16), V((n, rows, fpad + LANE), BF16),
        V((rows, features), F32), V((rows, 2 * NS), F32),
        V((kv_heads, 32, HEAD_SIZE), F32), V((kv_heads, 16, HEAD_SIZE), F32),
        V((kv_heads, 16, HEAD_SIZE), F32), V((kv_heads, 32, HEAD_SIZE), F32),
        V((16, NS), F32), V((16, m_heads * MP), F32),
        V((rows, round_up(outs) + opad + LANE), F32),
        V((n, rows, opad), BF16), V((n_short, n, rows, opad), BF16),
        V((n_short, total_rows, opad), F32),
        V((n_chunk, 2, n_short, half, fchunk), F32),
        V((n_chunk, 2, half, fchunk), BF16), V((n_chunk, 2, half, fchunk), BF16),
        V((n_chunk, n_short, half, fchunk), BF16),
        V((n_oc, n, rows, ochunk), BF16), V((n_oc, n, rows, ochunk), BF16),
        dma((4 + 2 * n_chunk + 3 + n_short + n_oc,)), dma((3,)),
        dma((n,)), dma((n,)), dma((2,)), dma((2,)), dma((n,)), dma((n,)),
        dma((n, n_short)), dma((n_short, n)), dma((n_chunk,)), dma((n_chunk,)),
        dma((n_chunk,)), dma((n_chunk,)), dma((n_oc, n)), dma((n_oc, n)),
    ]
    return pl.pallas_call(
        functools.partial(fused_kernel, dims),
        out_shape=jax.ShapeDtypeStruct((rows, width), BF16),
        in_specs=[vm, vm, vm, vm, vm, sm, vm, vm, vm] + [hb] * 10,
        out_specs=vm,
        scratch_shapes=scratch,
        name="layer",
        compiler_params=pltpu.CompilerParams(
            collective_id=0, has_side_effects=True, vmem_limit_bytes=66 * 1000 * 1000
        ),
    )(
        tokens, norm_gain[None, :], step_bias[None, :], decay_rate[None, :], skip_gain[None, :],
        lengths, cosf, sinf, mixer_gain[None, :],
        jnp.transpose(mixer_in, (1, 2, 0)), shared_in.T, step_in.T,
        cached_keys[0], cached_values[0], state_cache.reshape(m_heads * MP, NS),
        mixer_out, gate_weight, up_weight, down_weight,
    )


def fits(n, n_short, args):
    tokens, mixer_in, shared_in, step_in = args[0], args[2], args[3], args[4]
    return (
        n_short == 2
        and tokens.shape[0] == DRAFT_TOKENS
        and n * DRAFT_TOKENS == 32
        and mixer_in.shape[2] % 16 == 0
        and shared_in.shape[1] % 16 == 0
        and LANE % shared_in.shape[1] == 0
        and step_in.shape[1] % 16 == 0
        and args[13].shape[1] % 16 == 0
        and args[14].shape[1] % LANE == 0
    )


def layer(*args):
    if fits(lax.axis_size("wide"), lax.axis_size("short"), args):
        return fused(*args)
    return on_device(*args)


def solution(mesh):
    in_specs = (
        P(("groups", "wide"), "short"),
        P("short"),
        P("short", None, "wide"),
        P("short", "wide"),
        P("short", None),
        P("short"),
        P("short"),
        P("short"),
        P(("groups", "wide"), None, "short"),
        P(("groups", "wide"), None, "short"),
        P(("groups", "wide")),
        P(("groups", "wide"), "short", None, None),
        P("short"),
        P(None, "wide", "short"),
        P("short", "wide"),
        P("short", "wide"),
        P("wide", "short"),
    )
    out_specs = P(("groups", "wide"), "short")
    return jax.shard_map(
        layer, mesh=mesh, in_specs=in_specs, out_specs=out_specs, check_vma=False
    )
```

profile of v0, /device:TPU:0, one launch (start us, length us, event | category | flops | bytes accessed | tf_op | source)
XLA Modules:
  0.0 41.5 jit_solution(6570098755225208393)
XLA Ops:
  0.7 0.1 fusion
  0.8 0.7 %pad_maximum_fusion = (f32[4,128]{1,0:T(4,128)}, f32[4,128]{1,0:T(4,128)}) fusion(f32[4,64]{1,0:T(4,128)S(1)} %get-tuple-element.7, f32[4,64]{1,0:T(4,128)S(1)} %get-tuple-element.6, f32[4,64]{1,0:T(4,128)S(1)} %get-tuple-element.5), kind=kLoop, calls=%fused_computation.2 | loop fusion | flops 1024 | bytes 7168 | tf_op jit(solution)/shard_map/concatenate | solution.py:612
  1.5 1.3 %broadcast_in_dim.17.gain = f32[1,2560]{1,0:T(1,128)} reshape(f32[2560]{0:T(1024)} %param.18) | data formatting | bytes 20480 | tf_op jit(solution)/shard_map/broadcast_in_dim | solution.py:659
  2.8 37.4 %layer.1 = bf16[4,2560]{1,0:T(4,128)(2,1)} custom-call(bf16[4,2560]{1,0:T(4,128)(2,1)} %tokens.1, f32[1,2560]{1,0:T(1,128)} %broadcast_in_dim.17.gain, f32[1,16]{1,0:T(1,128)} %bitcast.19, f32[1,16]{1,0:T(1,128)} %bitcast.20, f32[1,16]{1,0:T(1,128)} %bitcast.21, s32[1]{0:T(128)} %copy.19.lengths, f32[4,128]{1,0:T(4,128)} %get-tuple-element.8.cosf, ...), custom_call_target="tpu_custom_call" | custom-call | tf_op jit(solution)/shard_map/layer/pallas_call | solution.py:648
  40.1 1.3 %copy.20 = bf16[4,2560]{1,0:T(4,128)(2,1)} copy(bf16[4,2560]{1,0:T(4,128)(2,1)} %layer.1) | data formatting | bytes 40960
  (2 shorter events, 0.0 us)
where the time goes:
time: 41.7 us; the launch traced here: 41.5 us
  Pallas kernels  37.4 us (90%)
  local copies, waits for them, and re-layouts  2.65 us (6%)
  other arithmetic  0.78 us (2%)
  between operations  0.67 us (2%)
    pallas_call x1, Pallas kernels, fused(): pl.pallas_call(functools.partial(fused_kernel, dims), out_shape=jax.Shape...  37.4 us
    unnamed x1, local copies, waits for them, and re-layouts  1.34 us
    broadcast_in_dim x1, local copies, waits for them, and re-layouts, fused(): norm_gain[None, :]  1.31 us

commit v1 on v0

--- a/solution.py
+++ b/solution.py
@@ -1,4 +1,5 @@
 import functools
+import math
 import jax
 import jax.numpy as jnp
 from jax import lax
@@ -241,11 +242,34 @@
     return lax.dot_general(a, b, NT, preferred_element_type=F32)
 
 
+def rope_rows(length, rows):
+    lane = lax.broadcasted_iota(jnp.int32, (rows, HEAD_SIZE), 1)
+    token = lax.broadcasted_iota(jnp.int32, (rows, HEAD_SIZE), 0)
+    pair = lax.rem(lane, HEAD_SIZE // 2).astype(F32)
+    angle = (token + length).astype(F32) * jnp.exp(pair * (-2.0 * math.log(10000.0) / HEAD_SIZE))
+    turns = jnp.floor(angle * (2.0 / math.pi) + 0.5)
+    rest = angle - turns * 1.5703125
+    rest = rest - turns * 4.837512969970703125e-4
+    rest = rest - turns * 7.54978995489188216e-8
+    z = rest * rest
+    sine = ((-1.9515295891e-4 * z + 8.3321608736e-3) * z - 1.6666654611e-1) * z * rest + rest
+    cosine = (2.443315711809948e-5 * z - 1.388731625493765e-3) * z + 4.166664568298827e-2
+    cosine = cosine * z * z - 0.5 * z + 1.0
+    quarter = turns - 4.0 * jnp.floor(turns * 0.25)
+    odd = (quarter == 1.0) | (quarter == 3.0)
+    cos_t = jnp.where(odd, sine, cosine)
+    cos_t = jnp.where((quarter == 1.0) | (quarter == 2.0), -cos_t, cos_t)
+    sin_t = jnp.where(odd, cosine, sine)
+    sin_t = jnp.where(quarter >= 2.0, -sin_t, sin_t)
+    return cos_t, jnp.where(lane < HEAD_SIZE // 2, -sin_t, sin_t)
+
+
 def fused_kernel(
     dims,
-    tokens, gain, bias, rate, skip, lengths, cosf, sinf, mixer_gain,
+    tokens, gain_h, bias_h, rate_h, skip_h, lengths_h, mixer_gain_h,
     mixer_in, shared_in, step_in, keys, values, state, mixer_out, gate, up, down,
     out,
+    gain, bias, rate, skip, lengths, mixer_gain,
     w_a, w_b, k_v, v_v, s_v, g_v, u_v, m_v, d_v,
     xg, xf, xb, sq_send, sq_recv, p_send, p_recv, c_b, tot, step_f,
     f_send, f_recv, feat, bc, qbuf, knbuf, vnbuf, obuf, cbuf, rbuf, own,
@@ -253,7 +277,9 @@
     sem_w, sem_loc, sem_gs, sem_gr, sem_ps, sem_pr, sem_fs, sem_fr,
     sem_ms, sem_mr, sem_us, sem_ur, sem_hs, sem_hr, sem_os, sem_or,
 ):
-    n, n_short, rows, width, gcol, scol, ncol, ocol, n_chunk, fchunk, n_oc, ochunk = dims
+    n, n_short, rows, width, gcol, scol, ncol, ocol, fspans, ospans = dims
+    n_chunk = len(fspans)
+    n_oc = len(ospans)
     total_rows = n * rows
     me = lax.axis_index("wide")
     s = lax.axis_index("short")
@@ -277,13 +303,6 @@
         weights.append(copy)
         return copy
 
-    fa = [
-        fetch(mixer_in.at[other], w_a.at[pl.ds(0, gcol)]),
-        fetch(shared_in, w_a.at[pl.ds(gcol, scol)]),
-        fetch(step_in, w_a.at[pl.ds(gcol + scol, ncol)]),
-    ]
-    fb = [fetch(mixer_in.at[s], w_b)]
-
     barrier = pltpu.get_barrier_semaphore()
     for d in range(n):
         for e in range(n_short):
@@ -293,37 +312,31 @@
                     device_id={"wide": peer(d), "short": lax.rem(s + e, n_short)},
                     device_id_type=MESH,
                 )
+    own_tokens = fetch(tokens, xg.at[me])
+    small = [
+        fetch(gain_h, gain), fetch(bias_h, bias), fetch(rate_h, rate), fetch(skip_h, skip),
+        fetch(lengths_h, lengths), fetch(mixer_gain_h, mixer_gain),
+    ]
+    fa = [
+        fetch(mixer_in.at[other], w_a.at[pl.ds(0, gcol)]),
+        fetch(shared_in, w_a.at[pl.ds(gcol, scol)]),
+        fetch(step_in, w_a.at[pl.ds(gcol + scol, ncol)]),
+    ]
+    fb = [fetch(mixer_in.at[s], w_b)]
 
     def cols(c):
-        return pl.ds(c * fchunk, fchunk)
+        return pl.ds(*fspans[c])
 
     fgu = []
     for c in range(n_chunk):
-        fgu.append((fetch(gate.at[:, cols(c)], g_v.at[c]), fetch(up.at[:, cols(c)], u_v.at[c])))
+        fgu.append(
+            (fetch(gate.at[:, cols(c)], g_v.at[:, cols(c)]), fetch(up.at[:, cols(c)], u_v.at[:, cols(c)]))
+        )
         if c == 0:
             fkv = [fetch(keys, k_v), fetch(values, v_v), fetch(state, s_v)]
+    fdn = [fetch(down.at[cols(c)], d_v.at[cols(c)]) for c in range(n_chunk)]
     fmo = [fetch(mixer_out.at[g], m_v.at[g, pl.ds(0, ocol)]) for g in range(n_short)]
-    fdn = [fetch(down.at[:, pl.ds(o * ochunk, ochunk)], d_v.at[o]) for o in range(n_oc)]
-
-    pl.semaphore_wait(barrier, n * n_short - 1)
-
-    def remote(src, dst, send, recv, wide, short):
-        copy = pltpu.make_async_remote_copy(
-            src_ref=src, dst_ref=dst, send_sem=send, recv_sem=recv,
-            device_id={"wide": wide, "short": short}, device_id_type=MESH,
-        )
-        copy.start()
-        return copy
-
-    def arrived(buf, recv):
-        pltpu.make_async_copy(buf, buf, recv).wait()
-
-    sent = []
-
-    for d in range(1, n):
-        sent.append(remote(tokens, xg.at[me], sem_gs.at[d], sem_gr.at[me], peer(d), s))
-    own_tokens = pltpu.make_async_copy(tokens, xg.at[me], sem_loc.at[0])
-    own_tokens.start()
+
     for g in range(n_short):
         if opad > ocol:
             m_v[g, ocol:opad, :] = jnp.zeros((opad - ocol, width), BF16)
@@ -337,6 +350,26 @@
     tot[...] = jnp.zeros_like(tot)
     own[...] = jnp.zeros_like(own)
     own_tokens.wait()
+    pl.semaphore_wait(barrier, n * n_short - 1)
+
+    def remote(src, dst, send, recv, wide, short):
+        copy = pltpu.make_async_remote_copy(
+            src_ref=src, dst_ref=dst, send_sem=send, recv_sem=recv,
+            device_id={"wide": wide, "short": short}, device_id_type=MESH,
+        )
+        copy.start()
+        return copy
+
+    def arrived(buf, recv):
+        pltpu.make_async_copy(buf, buf, recv).wait()
+
+    sent = []
+
+    for d in range(1, n):
+        sent.append(remote(xg.at[me], xg.at[me], sem_gs.at[d], sem_gr.at[me], peer(d), s))
+    for copy in small:
+        copy.wait()
+    cos_t, sin_t = rope_rows(lengths[...], rows)
     for d in range(1, n):
         arrived(xg.at[peer(d)], sem_gr.at[peer(d)])
     for j in range(n):
@@ -344,7 +377,9 @@
     x = xf[...]
     sq_send[...] = jnp.broadcast_to(jnp.sum(x * x, axis=1, keepdims=True), sq_send.shape)
     sent.append(remote(sq_send, sq_recv, sem_ps.at[0], sem_pr.at[0], me, other))
-    xb[...] = (x * gain[...]).astype(BF16)
+    for j in range(width // LANE):
+        lanes = slice(j * LANE, (j + 1) * LANE)
+        xb[:, lanes] = (xf[:, lanes] * gain[j : j + 1, :]).astype(BF16)
 
     for copy in fa:
         copy.wait()
@@ -378,35 +413,52 @@
     for d in range(1, n):
         to = peer(d)
         sent.append(remote(f_send.at[to], f_recv.at[me], sem_fs.at[d], sem_fr.at[me], to, s))
-    own_f = pltpu.make_async_copy(f_send.at[me], f_recv.at[me], sem_loc.at[1])
+    own_f = pltpu.make_async_copy(f_send.at[me], f_recv.at[me], sem_loc.at[0])
     own_f.start()
 
     half = total_rows // n_short
 
     def gate_up(c):
+        part = slice(fspans[c][0], fspans[c][0] + fspans[c][1])
         fgu[c][0].wait()
-        for i in range(n_short):
-            pass
-        both = [dot(xb[...], g_v[c])]
+        both = [dot(xb[...], g_v[:, part])]
         fgu[c][1].wait()
-        both.append(dot(xb[...], u_v[c]))
+        both.append(dot(xb[...], u_v[:, part]))
         for k in range(2):
             for i in range(n_short):
-                gsc[c, k, i] = both[k][half * i : half * (i + 1)] * inv[half * i : half * (i + 1)]
+                gsc[k, i, :, part] = both[k][half * i : half * (i + 1)] * inv[half * i : half * (i + 1)]
         for k in range(2):
-            gu_send[c, k] = gsc[c, k, other].astype(BF16)
-        sent.append(remote(gu_send.at[c], gu_recv.at[c], sem_us.at[c], sem_ur.at[c], me, other))
+            gu_send[k, :, part] = gsc[k, other, :, part].astype(BF16)
+        sent.append(
+            remote(
+                gu_send.at[:, :, cols(c)], gu_recv.at[:, :, cols(c)], sem_us.at[c], sem_ur.at[c], me, other
+            )
+        )
 
     def hidden(c):
-        arrived(gu_recv.at[c], sem_ur.at[c])
-        a = gsc[c, 0, s] + gu_recv[c, 0].astype(F32)
-        b = gsc[c, 1, s] + gu_recv[c, 1].astype(F32)
-        hbuf[c, s] = (silu(a) * b).astype(BF16)
+        part = slice(fspans[c][0], fspans[c][0] + fspans[c][1])
+        arrived(gu_recv.at[:, :, cols(c)], sem_ur.at[c])
+        a = gsc[0, s, :, part] + gu_recv[0, :, part].astype(F32)
+        b = gsc[1, s, :, part] + gu_recv[1, :, part].astype(F32)
+        hbuf[s, :, part] = (silu(a) * b).astype(BF16)
         sent.append(
-            remote(hbuf.at[c, s], hbuf.at[c, s], sem_hs.at[c], sem_hr.at[c], me, other)
+            remote(
+                hbuf.at[s, :, cols(c)], hbuf.at[s, :, cols(c)], sem_hs.at[c], sem_hr.at[c], me, other
+            )
         )
 
-    gate_up(0)
+    def down_part(c):
+        part = slice(fspans[c][0], fspans[c][0] + fspans[c][1])
+        arrived(hbuf.at[other, :, cols(c)], sem_hr.at[c])
+        fdn[c].wait()
+        term = dot(hbuf[:, :, part].reshape(total_rows, fspans[c][1]), d_v[part, :])
+        xf[...] = term if c == 0 else xf[...] + term
+
+    early = max(1, n_chunk - 1)
+    for c in range(early):
+        gate_up(c)
+        if c:
+            hidden(c - 1)
 
     own_f.wait()
     for d in range(1, n):
@@ -424,13 +476,11 @@
     v_at = k_at + kv_heads * HEAD_SIZE
     x_at = v_at + kv_heads * HEAD_SIZE
     z_at = x_at + m_heads * MP
-    cos_t = cosf[...]
-    sin_t = sinf[...]
 
     def turn(v):
         return v * cos_t + jnp.concatenate([v[:, HEAD_SIZE // 2 :], v[:, : HEAD_SIZE // 2]], axis=1) * sin_t
 
-    length = lengths[0]
+    length = lengths[...]
     for kv in range(kv_heads):
         for i in range(rep):
             h = kv * rep + i
@@ -512,14 +562,16 @@
                         to, lax.rem(s + e, n_short),
                     )
                 )
-    own_m = pltpu.make_async_copy(m_send.at[me], m_recv.at[s, me], sem_loc.at[2])
+    own_m = pltpu.make_async_copy(m_send.at[me], m_recv.at[s, me], sem_loc.at[1])
     own_m.start()
 
-    hidden(0)
-    for c in range(1, n_chunk):
+    for c in range(early, n_chunk):
         gate_up(c)
-        if c > 1:
-            hidden(c - 1)
+        hidden(c - 1)
+    for c in range(n_chunk):
+        if c == max(0, n_chunk - 2):
+            hidden(n_chunk - 1)
+        down_part(c)
     own_m.wait()
     for d in range(n):
         for e in range(n_short):
@@ -529,38 +581,31 @@
     for g in range(n_short):
         for j in range(n):
             lhs[g, rows * j : rows * (j + 1), :] = m_recv[g, j].astype(F32)
-    if n_chunk > 1:
-        hidden(n_chunk - 1)
     for copy in fmo:
         copy.wait()
-    for c in range(n_chunk):
-        arrived(hbuf.at[c, other], sem_hr.at[c])
     for o in range(n_oc):
-        oc = slice(o * ochunk, (o + 1) * ochunk)
-        acc = dot(lhs[0].astype(BF16), m_v[0, :, oc])
-        for g in range(1, n_short):
+        oc = slice(ospans[o][0], ospans[o][0] + ospans[o][1])
+        acc = xf[:, oc]
+        for g in range(n_short):
             acc = acc + dot(lhs[g].astype(BF16), m_v[g, :, oc])
-        fdn[o].wait()
-        for c in range(n_chunk):
-            acc = acc + dot(
-                hbuf[c].reshape(total_rows, fchunk), d_v[o, c * fchunk : (c + 1) * fchunk, :]
-            )
         xf[:, oc] = acc
         for r in range(n):
-            o_send[o, r] = xf[rows * r : rows * (r + 1), oc].astype(BF16)
-        for d in range(1, n):
-            to = peer(d)
+            o_send[r, :, oc] = xf[rows * r : rows * (r + 1), oc].astype(BF16)
+        for k in range(n - 1):
+            to = jnp.where(me <= k, k + 1, k)
+            part = pl.ds(*ospans[o])
             sent.append(
                 remote(
-                    o_send.at[o, to], o_recv.at[o, me], sem_os.at[o, d], sem_or.at[o, me], to, s
+                    o_send.at[to, :, part], o_recv.at[me, :, part], sem_os.at[o, k], sem_or.at[o, me], to, s
                 )
             )
     for o in range(n_oc):
-        oc = slice(o * ochunk, (o + 1) * ochunk)
-        acc = tokens[:, oc].astype(F32) + o_send[o, me].astype(F32)
+        part = pl.ds(*ospans[o])
+        oc = slice(ospans[o][0], ospans[o][0] + ospans[o][1])
+        acc = xg[me, :, oc].astype(F32) + o_send[me, :, oc].astype(F32)
         for d in range(1, n):
-            arrived(o_recv.at[o, peer(d)], sem_or.at[o, peer(d)])
-            acc = acc + o_recv[o, peer(d)].astype(F32)
+            arrived(o_recv.at[peer(d), :, part], sem_or.at[o, peer(d)])
+            acc = acc + o_recv[peer(d), :, oc].astype(F32)
         out[:, oc] = acc.astype(BF16)
     for copy in sent:
         copy.wait_send()
@@ -574,12 +619,8 @@
     return round_up(gcol + LANE - 1)
 
 
-def pieces_of(width, most):
-    tiles = width // LANE
-    for k in range(most, 0, -1):
-        if tiles % k == 0:
-            return k
-    return 1
+def spans_of(width, piece):
+    return tuple((at, min(piece, width - at)) for at in range(0, width, piece))
 
 
 def fused(*args):
@@ -594,10 +635,10 @@
     ncol = step_in.shape[1]
     ocol = mixer_out.shape[1]
     ffl = gate_weight.shape[1]
-    n_chunk = pieces_of(ffl, 3)
-    fchunk = ffl // n_chunk
-    n_oc = pieces_of(width, 4)
-    ochunk = width // n_oc
+    fspans = spans_of(ffl, 1024)
+    ospans = spans_of(width, 512)
+    n_chunk = len(fspans)
+    n_oc = len(ospans)
     m_heads = MH // n_short
     kv_heads = KEY_VALUE_HEADS // n_short
     total_rows = n * rows
@@ -607,23 +648,20 @@
     features = n * gcol
     outs = n * ocol
     half = total_rows // n_short
-    positions = lengths + jnp.arange(rows, dtype=jnp.int32)
-    cos_table, sin_table = rope_tables(positions)
-    cosf = jnp.concatenate([cos_table, cos_table], axis=-1)
-    sinf = jnp.concatenate([-sin_table, sin_table], axis=-1)
-    dims = (n, n_short, rows, width, gcol, scol, ncol, ocol, n_chunk, fchunk, n_oc, ochunk)
+    dims = (n, n_short, rows, width, gcol, scol, ncol, ocol, fspans, ospans)
     vm = pl.BlockSpec(memory_space=pltpu.VMEM)
-    sm = pl.BlockSpec(memory_space=pltpu.SMEM)
     hb = pl.BlockSpec(memory_space=pl.ANY)
     V = pltpu.VMEM
     dma = pltpu.SemaphoreType.DMA
     kvw = cached_keys.shape[2]
     slots = cached_keys.shape[1]
     scratch = [
+        V((width // LANE, LANE), F32), V((1, m_heads), F32), V((1, m_heads), F32),
+        V((1, m_heads), F32), V((1, 1), jnp.int32), V((1, m_heads * MP), F32),
         V((acol, width), BF16), V((gcol, width), BF16), V((slots, kvw), BF16),
         V((slots, kvw), BF16), V((m_heads * MP, NS), BF16),
-        V((n_chunk, width, fchunk), BF16), V((n_chunk, width, fchunk), BF16),
-        V((n_short, opad, width), BF16), V((n_oc, ffl, ochunk), BF16),
+        V((width, ffl), BF16), V((width, ffl), BF16),
+        V((n_short, opad, width), BF16), V((ffl, width), BF16),
         V((n, rows, width), BF16), V((total_rows, width), F32), V((total_rows, width), BF16),
         V((total_rows, LANE), F32), V((total_rows, LANE), F32),
         V((total_rows, acol), F32), V((total_rows, acol), F32), V((total_rows, fpad), F32),
@@ -636,19 +674,19 @@
         V((rows, round_up(outs) + opad + LANE), F32),
         V((n, rows, opad), BF16), V((n_short, n, rows, opad), BF16),
         V((n_short, total_rows, opad), F32),
-        V((n_chunk, 2, n_short, half, fchunk), F32),
-        V((n_chunk, 2, half, fchunk), BF16), V((n_chunk, 2, half, fchunk), BF16),
-        V((n_chunk, n_short, half, fchunk), BF16),
-        V((n_oc, n, rows, ochunk), BF16), V((n_oc, n, rows, ochunk), BF16),
-        dma((4 + 2 * n_chunk + 3 + n_short + n_oc,)), dma((3,)),
+        V((2, n_short, half, ffl), F32),
+        V((2, half, ffl), BF16), V((2, half, ffl), BF16),
+        V((n_short, half, ffl), BF16),
+        V((n, rows, width), BF16), V((n, rows, width), BF16),
+        dma((7 + 4 + 3 * n_chunk + 3 + n_short,)), dma((2,)),
         dma((n,)), dma((n,)), dma((2,)), dma((2,)), dma((n,)), dma((n,)),
         dma((n, n_short)), dma((n_short, n)), dma((n_chunk,)), dma((n_chunk,)),
         dma((n_chunk,)), dma((n_chunk,)), dma((n_oc, n)), dma((n_oc, n)),
     ]
     return pl.pallas_call(
         functools.partial(fused_kernel, dims),
-        out_shape=jax.ShapeDtypeStruct((rows, width), BF16),
-        in_specs=[vm, vm, vm, vm, vm, sm, vm, vm, vm] + [hb] * 10,
+        out_shape=pltpu.VMEM((rows, width), BF16),
+        in_specs=[hb] * 17,
         out_specs=vm,
         scratch_shapes=scratch,
         name="layer",
@@ -656,8 +694,8 @@
             collective_id=0, has_side_effects=True, vmem_limit_bytes=66 * 1000 * 1000
         ),
     )(
-        tokens, norm_gain[None, :], step_bias[None, :], decay_rate[None, :], skip_gain[None, :],
-        lengths, cosf, sinf, mixer_gain[None, :],
+        tokens, norm_gain.reshape(width // LANE, LANE), step_bias[None, :], decay_rate[None, :],
+        skip_gain[None, :], lengths[None, :], mixer_gain[None, :],
         jnp.transpose(mixer_in, (1, 2, 0)), shared_in.T, step_in.T,
         cached_keys[0], cached_values[0], state_cache.reshape(m_heads * MP, NS),
         mixer_out, gate_weight, up_weight, down_weight,
@@ -676,6 +714,7 @@
         and step_in.shape[1] % 16 == 0
         and args[13].shape[1] % 16 == 0
         and args[14].shape[1] % LANE == 0
+        and tokens.shape[1] % LANE == 0
     )
 
 

time: 41.7 us -> 34.6 us (0.83)
  Pallas kernels: 37.4 us -> 33.2 us
  local copies, waits for them, and re-layouts: 2.65 us -> 0.61 us
  other arithmetic: 0.78 us -> 0 us
    pallas_call x1, Pallas kernels: 37.4 us -> 33.2 us  [fused(): pl.pallas_call(functools.partial(fused_kernel, dims), out_shape=pltpu.VME...]
    broadcast_in_dim x1 -> x0, local copies, waits for them, and re-layouts: 1.31 us -> none  [fused(): norm_gain[None, :]]
    unnamed x1, local copies, waits for them, and re-layouts: 1.34 us -> 0.61 us
    concatenate x1 -> x0, other arithmetic: 0.66 us -> none  [fused(): cosf = jnp.concatenate([cos_table, cos_table], axis=-1)]
where the time goes in v1:
time: 34.6 us; the launch traced here: 34.5 us
  Pallas kernels  33.2 us (96%)
  between operations  0.66 us (2%)
  local copies, waits for them, and re-layouts  0.61 us (2%)
    pallas_call x1, Pallas kernels, fused(): pl.pallas_call(functools.partial(fused_kernel, dims), out_shape=pltpu.VME...  33.2 us

profile of v1, /device:TPU:0, one launch (start us, length us, event | category | flops | bytes accessed | tf_op | source)
XLA Modules:
  0.0 34.5 jit_solution(3927162499803719042)
XLA Ops:
  0.7 33.2 %layer.1 = bf16[4,2560]{1,0:T(4,128)(2,1)S(1)} custom-call(bf16[4,2560]{1,0:T(4,128)(2,1)} %tokens.1, f32[20,128]{1,0:T(8,128)} %bitcast.19, f32[1,16]{1,0:T(1,128)} %bitcast.21, f32[1,16]{1,0:T(1,128)} %bitcast.22, f32[1,16]{1,0:T(1,128)} %bitcast.23, s32[1,1]{1,0:T(1,128)} %bitcast.12.lengths_h, f32[1,2048]{1,0:T(1,128)} %bitcast.20, ...), custom_call_target="tpu_custom_call" | custom-call | tf_op jit(solution)/shard_map/layer/pallas_call | solution.py:686
  33.9 0.6 %copy.19 = bf16[4,2560]{1,0:T(4,128)(2,1)} copy(bf16[4,2560]{1,0:T(4,128)(2,1)S(1)} %layer.1) | data formatting | bytes 40960

commit v2 on v1

--- a/solution.py
+++ b/solution.py
@@ -266,10 +266,10 @@
 
 def fused_kernel(
     dims,
-    tokens, gain_h, bias_h, rate_h, skip_h, lengths_h, mixer_gain_h,
+    tokens, gain_h, bias_h, rate_h, skip_h, lengths, mixer_gain_h,
     mixer_in, shared_in, step_in, keys, values, state, mixer_out, gate, up, down,
     out,
-    gain, bias, rate, skip, lengths, mixer_gain,
+    gain, bias, rate, skip, mixer_gain,
     w_a, w_b, k_v, v_v, s_v, g_v, u_v, m_v, d_v,
     xg, xf, xb, sq_send, sq_recv, p_send, p_recv, c_b, tot, step_f,
     f_send, f_recv, feat, bc, qbuf, knbuf, vnbuf, obuf, cbuf, rbuf, own,
@@ -295,6 +295,13 @@
     def peer(d):
         return lax.rem(me + d, n)
 
+    def upward(k):
+        return jnp.where(me <= k, k + 1, k)
+
+    def far_first(k):
+        down_to = n - 1 - k
+        return jnp.where(2 * me >= n, upward(k), jnp.where(down_to > me, down_to, down_to - 1))
+
     weights = []
 
     def fetch(src, dst):
@@ -304,18 +311,20 @@
         return copy
 
     barrier = pltpu.get_barrier_semaphore()
-    for d in range(n):
+    for k in range(n):
         for e in range(n_short):
-            if d or e:
+            if k < n - 1 or e:
                 pl.semaphore_signal(
                     barrier, inc=1,
-                    device_id={"wide": peer(d), "short": lax.rem(s + e, n_short)},
+                    device_id={
+                        "wide": far_first(k) if k < n - 1 else me, "short": lax.rem(s + e, n_short)
+                    },
                     device_id_type=MESH,
                 )
     own_tokens = fetch(tokens, xg.at[me])
     small = [
         fetch(gain_h, gain), fetch(bias_h, bias), fetch(rate_h, rate), fetch(skip_h, skip),
-        fetch(lengths_h, lengths), fetch(mixer_gain_h, mixer_gain),
+        fetch(mixer_gain_h, mixer_gain),
     ]
     fa = [
         fetch(mixer_in.at[other], w_a.at[pl.ds(0, gcol)]),
@@ -365,13 +374,12 @@
 
     sent = []
 
-    for d in range(1, n):
-        sent.append(remote(xg.at[me], xg.at[me], sem_gs.at[d], sem_gr.at[me], peer(d), s))
+    for k in range(n - 1):
+        remote(xg.at[me], xg.at[me], sem_gs, sem_gr, far_first(k), s)
     for copy in small:
         copy.wait()
-    cos_t, sin_t = rope_rows(lengths[...], rows)
-    for d in range(1, n):
-        arrived(xg.at[peer(d)], sem_gr.at[peer(d)])
+    cos_t, sin_t = rope_rows(lengths[0], rows)
+    arrived(xg.at[pl.ds(0, n - 1)], sem_gr)
     for j in range(n):
         xf[rows * j : rows * (j + 1), :] = xg[j].astype(F32)
     x = xf[...]
@@ -410,9 +418,9 @@
     for r in range(n):
         f_send[r, :, :fpad] = tot[rows * r : rows * (r + 1), :].astype(BF16)
         f_send[r, :, fpad:] = c_b[rows * r : rows * (r + 1), :LANE].astype(BF16)
-    for d in range(1, n):
-        to = peer(d)
-        sent.append(remote(f_send.at[to], f_recv.at[me], sem_fs.at[d], sem_fr.at[me], to, s))
+    for k in range(n - 1):
+        to = far_first(k)
+        remote(f_send.at[to], f_recv.at[me], sem_fs, sem_fr, to, s)
     own_f = pltpu.make_async_copy(f_send.at[me], f_recv.at[me], sem_loc.at[0])
     own_f.start()
 
@@ -461,8 +469,7 @@
             hidden(c - 1)
 
     own_f.wait()
-    for d in range(1, n):
-        arrived(f_recv.at[peer(d)], sem_fr.at[peer(d)])
+    arrived(f_recv.at[pl.ds(0, n - 1)], sem_fr)
     fwidth = feat.shape[1]
     for j in range(n):
         base = gcol * j // LANE * LANE
@@ -480,7 +487,7 @@
     def turn(v):
         return v * cos_t + jnp.concatenate([v[:, HEAD_SIZE // 2 :], v[:, : HEAD_SIZE // 2]], axis=1) * sin_t
 
-    length = lengths[...]
+    length = lengths[0]
     for kv in range(kv_heads):
         for i in range(rep):
             h = kv * rep + i
@@ -552,17 +559,14 @@
         if off:
             v = jnp.concatenate([v[:, off:], v[:, :off]], axis=1)
         m_send[j] = v[:, :opad].astype(BF16)
-    for d in range(n):
-        to = peer(d)
+    for k in range(n):
+        to = far_first(k) if k < n - 1 else me
         for e in range(n_short):
-            if d or e:
-                sent.append(
-                    remote(
-                        m_send.at[to], m_recv.at[s, me], sem_ms.at[d, e], sem_mr.at[s, me],
-                        to, lax.rem(s + e, n_short),
-                    )
+            if k < n - 1 or e:
+                remote(
+                    m_send.at[to], m_recv.at[s * n + me], sem_ms, sem_mr, to, lax.rem(s + e, n_short)
                 )
-    own_m = pltpu.make_async_copy(m_send.at[me], m_recv.at[s, me], sem_loc.at[1])
+    own_m = pltpu.make_async_copy(m_send.at[me], m_recv.at[s * n + me], sem_loc.at[1])
     own_m.start()
 
     for c in range(early, n_chunk):
@@ -573,14 +577,10 @@
             hidden(n_chunk - 1)
         down_part(c)
     own_m.wait()
-    for d in range(n):
-        for e in range(n_short):
-            if d or e:
-                g = lax.rem(s + e, n_short)
-                arrived(m_recv.at[g, peer(d)], sem_mr.at[g, peer(d)])
+    arrived(m_recv.at[pl.ds(0, n * n_short - 1)], sem_mr)
     for g in range(n_short):
         for j in range(n):
-            lhs[g, rows * j : rows * (j + 1), :] = m_recv[g, j].astype(F32)
+            lhs[g, rows * j : rows * (j + 1), :] = m_recv[g * n + j].astype(F32)
     for copy in fmo:
         copy.wait()
     for o in range(n_oc):
@@ -592,23 +592,24 @@
         for r in range(n):
             o_send[r, :, oc] = xf[rows * r : rows * (r + 1), oc].astype(BF16)
         for k in range(n - 1):
-            to = jnp.where(me <= k, k + 1, k)
+            to = upward(k)
             part = pl.ds(*ospans[o])
-            sent.append(
-                remote(
-                    o_send.at[to, :, part], o_recv.at[me, :, part], sem_os.at[o, k], sem_or.at[o, me], to, s
-                )
-            )
+            remote(o_send.at[to, :, part], o_recv.at[me, :, part], sem_os.at[o], sem_or.at[o], to, s)
     for o in range(n_oc):
         part = pl.ds(*ospans[o])
         oc = slice(ospans[o][0], ospans[o][0] + ospans[o][1])
         acc = xg[me, :, oc].astype(F32) + o_send[me, :, oc].astype(F32)
+        arrived(o_recv.at[pl.ds(0, n - 1), :, part], sem_or.at[o])
         for d in range(1, n):
-            arrived(o_recv.at[peer(d), :, part], sem_or.at[o, peer(d)])
             acc = acc + o_recv[peer(d), :, oc].astype(F32)
         out[:, oc] = acc.astype(BF16)
     for copy in sent:
         copy.wait_send()
+    arrived(xg.at[pl.ds(0, n - 1)], sem_gs)
+    arrived(f_send.at[pl.ds(0, n - 1)], sem_fs)
+    arrived(m_recv.at[pl.ds(0, n * n_short - 1)], sem_ms)
+    for o in range(n_oc):
+        arrived(o_send.at[pl.ds(0, n - 1), :, pl.ds(*ospans[o])], sem_os.at[o])
 
 
 def round_up(v):
@@ -636,7 +637,8 @@
     ocol = mixer_out.shape[1]
     ffl = gate_weight.shape[1]
     fspans = spans_of(ffl, 1024)
-    ospans = spans_of(width, 512)
+    first = min(512, width)
+    ospans = ((0, first),) + tuple((first + at, size) for at, size in spans_of(width - first, 1024))
     n_chunk = len(fspans)
     n_oc = len(ospans)
     m_heads = MH // n_short
@@ -657,7 +659,7 @@
     slots = cached_keys.shape[1]
     scratch = [
         V((width // LANE, LANE), F32), V((1, m_heads), F32), V((1, m_heads), F32),
-        V((1, m_heads), F32), V((1, 1), jnp.int32), V((1, m_heads * MP), F32),
+        V((1, m_heads), F32), V((1, m_heads * MP), F32),
         V((acol, width), BF16), V((gcol, width), BF16), V((slots, kvw), BF16),
         V((slots, kvw), BF16), V((m_heads * MP, NS), BF16),
         V((width, ffl), BF16), V((width, ffl), BF16),
@@ -672,21 +674,21 @@
         V((kv_heads, 16, HEAD_SIZE), F32), V((kv_heads, 32, HEAD_SIZE), F32),
         V((16, NS), F32), V((16, m_heads * MP), F32),
         V((rows, round_up(outs) + opad + LANE), F32),
-        V((n, rows, opad), BF16), V((n_short, n, rows, opad), BF16),
+        V((n, rows, opad), BF16), V((n_short * n, rows, opad), BF16),
         V((n_short, total_rows, opad), F32),
         V((2, n_short, half, ffl), F32),
         V((2, half, ffl), BF16), V((2, half, ffl), BF16),
         V((n_short, half, ffl), BF16),
         V((n, rows, width), BF16), V((n, rows, width), BF16),
-        dma((7 + 4 + 3 * n_chunk + 3 + n_short,)), dma((2,)),
-        dma((n,)), dma((n,)), dma((2,)), dma((2,)), dma((n,)), dma((n,)),
-        dma((n, n_short)), dma((n_short, n)), dma((n_chunk,)), dma((n_chunk,)),
-        dma((n_chunk,)), dma((n_chunk,)), dma((n_oc, n)), dma((n_oc, n)),
+        dma((6 + 4 + 3 * n_chunk + 3 + n_short,)), dma((2,)),
+        dma, dma, dma((2,)), dma((2,)), dma, dma,
+        dma, dma, dma((n_chunk,)), dma((n_chunk,)),
+        dma((n_chunk,)), dma((n_chunk,)), dma((n_oc,)), dma((n_oc,)),
     ]
     return pl.pallas_call(
         functools.partial(fused_kernel, dims),
         out_shape=pltpu.VMEM((rows, width), BF16),
-        in_specs=[hb] * 17,
+        in_specs=[hb] * 5 + [pl.BlockSpec(memory_space=pltpu.SMEM)] + [hb] * 11,
         out_specs=vm,
         scratch_shapes=scratch,
         name="layer",
@@ -695,7 +697,7 @@
         ),
     )(
         tokens, norm_gain.reshape(width // LANE, LANE), step_bias[None, :], decay_rate[None, :],
-        skip_gain[None, :], lengths[None, :], mixer_gain[None, :],
+        skip_gain[None, :], lengths, mixer_gain[None, :],
         jnp.transpose(mixer_in, (1, 2, 0)), shared_in.T, step_in.T,
         cached_keys[0], cached_values[0], state_cache.reshape(m_heads * MP, NS),
         mixer_out, gate_weight, up_weight, down_weight,

time: 34.6 us -> 32.7 us (0.945)
  Pallas kernels: 33.2 us -> 31.3 us
    pallas_call x1, Pallas kernels: 33.2 us -> 31.3 us  [fused(): pl.pallas_call(functools.partial(fused_kernel, dims), out_shape=pltpu.VME...]
where the time goes in v2:
time: 32.7 us; the launch traced here: 32.5 us
  Pallas kernels  31.3 us (96%)
  between operations  0.66 us (2%)
  local copies, waits for them, and re-layouts  0.61 us (2%)
    pallas_call x1, Pallas kernels, fused(): pl.pallas_call(functools.partial(fused_kernel, dims), out_shape=pltpu.VME...  31.3 us

profile of v2, /device:TPU:0, one launch (start us, length us, event | category | flops | bytes accessed | tf_op | source)
XLA Modules:
  0.0 32.5 jit_solution(18346382488185496106)
XLA Ops:
  0.7 31.3 %layer.1 = bf16[4,2560]{1,0:T(4,128)(2,1)S(1)} custom-call(bf16[4,2560]{1,0:T(4,128)(2,1)} %tokens.1, f32[20,128]{1,0:T(8,128)} %bitcast.17, f32[1,16]{1,0:T(1,128)} %bitcast.19, f32[1,16]{1,0:T(1,128)} %bitcast.20, f32[1,16]{1,0:T(1,128)} %bitcast.21, s32[1]{0:T(128)S(6)} %copy.20.lengths, f32[1,2048]{1,0:T(1,128)} %bitcast.18, ...), custom_call_target="tpu_custom_call" | custom-call | tf_op jit(solution)/shard_map/layer/pallas_call | solution.py:688
  31.9 0.6 %copy.19 = bf16[4,2560]{1,0:T(4,128)(2,1)} copy(bf16[4,2560]{1,0:T(4,128)(2,1)S(1)} %layer.1) | data formatting | bytes 40960

commit v3 on v2

--- a/solution.py
+++ b/solution.py
@@ -326,12 +326,14 @@
         fetch(gain_h, gain), fetch(bias_h, bias), fetch(rate_h, rate), fetch(skip_h, skip),
         fetch(mixer_gain_h, mixer_gain),
     ]
+    lead = dims_lead(gcol)
     fa = [
-        fetch(mixer_in.at[other], w_a.at[pl.ds(0, gcol)]),
-        fetch(shared_in, w_a.at[pl.ds(gcol, scol)]),
-        fetch(step_in, w_a.at[pl.ds(gcol + scol, ncol)]),
+        fetch(mixer_in.at[s, pl.ds(0, lead)], w_a.at[pl.ds(0, lead)]),
+        fetch(mixer_in.at[other], w_a.at[pl.ds(lead, gcol)]),
+        fetch(shared_in, w_a.at[pl.ds(lead + gcol, scol)]),
+        fetch(step_in, w_a.at[pl.ds(lead + gcol + scol, ncol)]),
     ]
-    fb = [fetch(mixer_in.at[s], w_b)]
+    fb = [fetch(mixer_in.at[s, pl.ds(lead, gcol - lead)], w_b)]
 
     def cols(c):
         return pl.ds(*fspans[c])
@@ -346,6 +348,24 @@
     fdn = [fetch(down.at[cols(c)], d_v.at[cols(c)]) for c in range(n_chunk)]
     fmo = [fetch(mixer_out.at[g], m_v.at[g, pl.ds(0, ocol)]) for g in range(n_short)]
 
+    own_tokens.wait()
+    pl.semaphore_wait(barrier, n * n_short - 1)
+
+    def remote(src, dst, send, recv, wide, short):
+        copy = pltpu.make_async_remote_copy(
+            src_ref=src, dst_ref=dst, send_sem=send, recv_sem=recv,
+            device_id={"wide": wide, "short": short}, device_id_type=MESH,
+        )
+        copy.start()
+        return copy
+
+    def arrived(buf, recv):
+        pltpu.make_async_copy(buf, buf, recv).wait()
+
+    sent = []
+
+    for k in range(n - 1):
+        remote(xg.at[me], xg.at[me], sem_gs, sem_gr, far_first(k), s)
     for g in range(n_short):
         if opad > ocol:
             m_v[g, ocol:opad, :] = jnp.zeros((opad - ocol, width), BF16)
@@ -358,24 +378,6 @@
     c_b[...] = jnp.zeros_like(c_b)
     tot[...] = jnp.zeros_like(tot)
     own[...] = jnp.zeros_like(own)
-    own_tokens.wait()
-    pl.semaphore_wait(barrier, n * n_short - 1)
-
-    def remote(src, dst, send, recv, wide, short):
-        copy = pltpu.make_async_remote_copy(
-            src_ref=src, dst_ref=dst, send_sem=send, recv_sem=recv,
-            device_id={"wide": wide, "short": short}, device_id_type=MESH,
-        )
-        copy.start()
-        return copy
-
-    def arrived(buf, recv):
-        pltpu.make_async_copy(buf, buf, recv).wait()
-
-    sent = []
-
-    for k in range(n - 1):
-        remote(xg.at[me], xg.at[me], sem_gs, sem_gr, far_first(k), s)
     for copy in small:
         copy.wait()
     cos_t, sin_t = rope_rows(lengths[0], rows)
@@ -391,10 +393,12 @@
 
     for copy in fa:
         copy.wait()
-    p_send[...] = dot_nt(xb[...], w_a[...])
+    both = dot_nt(xb[...], w_a[...])
+    p_send[...] = both[:, lead:]
+    c_b[:, :lead] = both[:, :lead]
     sent.append(remote(p_send, p_recv, sem_ps.at[1], sem_pr.at[1], me, other))
     fb[0].wait()
-    c_b[:, :gcol] = dot_nt(xb[...], w_b[...])
+    c_b[:, lead:gcol] = dot_nt(xb[...], w_b[...])
     lane = lax.broadcasted_iota(jnp.int32, (total_rows, acol), 1)
     mine = jnp.where(lane < gcol, c_b[:, :acol], p_send[...])
     arrived(sq_recv, sem_pr.at[0])
@@ -510,9 +514,9 @@
         old = jnp.exp(old - top)
         new = jnp.exp(new - top)
         den = jnp.sum(old, axis=1, keepdims=True) + jnp.sum(new, axis=1, keepdims=True)
-        obuf[kv] = dot((old / den).astype(BF16), v_v[:, head]) + dot(
-            (new / den).astype(BF16), vnbuf[kv].astype(BF16)
-        )
+        obuf[kv] = (
+            dot(old.astype(BF16), v_v[:, head]) + dot(new.astype(BF16), vnbuf[kv].astype(BF16))
+        ) / den
         for i in range(rep):
             h = kv * rep + i
             own[:, h * HEAD_SIZE : (h + 1) * HEAD_SIZE] = obuf[kv, rows * i : rows * (i + 1), :]
@@ -583,6 +587,11 @@
             lhs[g, rows * j : rows * (j + 1), :] = m_recv[g * n + j].astype(F32)
     for copy in fmo:
         copy.wait()
+    def out_to(o, k):
+        to = upward(k)
+        part = pl.ds(*ospans[o])
+        remote(o_send.at[to, :, part], o_recv.at[me, :, part], sem_os.at[o], sem_or.at[o], to, s)
+
     for o in range(n_oc):
         oc = slice(ospans[o][0], ospans[o][0] + ospans[o][1])
         acc = xf[:, oc]
@@ -591,10 +600,12 @@
         xf[:, oc] = acc
         for r in range(n):
             o_send[r, :, oc] = xf[rows * r : rows * (r + 1), oc].astype(BF16)
-        for k in range(n - 1):
-            to = upward(k)
-            part = pl.ds(*ospans[o])
-            remote(o_send.at[to, :, part], o_recv.at[me, :, part], sem_os.at[o], sem_or.at[o], to, s)
+        out_to(o, 0)
+        if o:
+            for k in range(1, n - 1):
+                out_to(o - 1, k)
+    for k in range(1, n - 1):
+        out_to(n_oc - 1, k)
     for o in range(n_oc):
         part = pl.ds(*ospans[o])
         oc = slice(ospans[o][0], ospans[o][0] + ospans[o][1])
@@ -614,6 +625,10 @@
 
 def round_up(v):
     return -(-v // LANE) * LANE
+
+
+def dims_lead(gcol):
+    return min(LANE, gcol - 16)
 
 
 def xpad(gcol):
@@ -647,6 +662,7 @@
     acol = gcol + scol + ncol
     fpad = xpad(gcol)
     opad = round_up(ocol)
+    lead = dims_lead(gcol)
     features = n * gcol
     outs = n * ocol
     half = total_rows // n_short
@@ -660,7 +676,7 @@
     scratch = [
         V((width // LANE, LANE), F32), V((1, m_heads), F32), V((1, m_heads), F32),
         V((1, m_heads), F32), V((1, m_heads * MP), F32),
-        V((acol, width), BF16), V((gcol, width), BF16), V((slots, kvw), BF16),
+        V((lead + acol, width), BF16), V((gcol - lead, width), BF16), V((slots, kvw), BF16),
         V((slots, kvw), BF16), V((m_heads * MP, NS), BF16),
         V((width, ffl), BF16), V((width, ffl), BF16),
         V((n_short, opad, width), BF16), V((ffl, width), BF16),
@@ -680,7 +696,7 @@
         V((2, half, ffl), BF16), V((2, half, ffl), BF16),
         V((n_short, half, ffl), BF16),
         V((n, rows, width), BF16), V((n, rows, width), BF16),
-        dma((6 + 4 + 3 * n_chunk + 3 + n_short,)), dma((2,)),
+        dma((6 + 5 + 3 * n_chunk + 3 + n_short,)), dma((2,)),
         dma, dma, dma((2,)), dma((2,)), dma, dma,
         dma, dma, dma((n_chunk,)), dma((n_chunk,)),
         dma((n_chunk,)), dma((n_chunk,)), dma((n_oc,)), dma((n_oc,)),

time: 32.7 us -> 31.8 us (0.972)
  Pallas kernels: 31.3 us -> 30.4 us
    pallas_call x1, Pallas kernels: 31.3 us -> 30.4 us  [fused(): pl.pallas_call(functools.partial(fused_kernel, dims), out_shape=pltpu.VME...]
where the time goes in v3:
time: 31.8 us; the launch traced here: 31.6 us
  Pallas kernels  30.4 us (96%)
  between operations  0.66 us (2%)
  local copies, waits for them, and re-layouts  0.61 us (2%)
    pallas_call x1, Pallas kernels, fused(): pl.pallas_call(functools.partial(fused_kernel, dims), out_shape=pltpu.VME...  30.4 us

profile of v3, /device:TPU:0, one launch (start us, length us, event | category | flops | bytes accessed | tf_op | source)
XLA Modules:
  0.0 31.6 jit_solution(515602665995190028)
XLA Ops:
  0.7 30.4 %layer.1 = bf16[4,2560]{1,0:T(4,128)(2,1)S(1)} custom-call(bf16[4,2560]{1,0:T(4,128)(2,1)} %tokens.1, f32[20,128]{1,0:T(8,128)} %bitcast.17, f32[1,16]{1,0:T(1,128)} %bitcast.19, f32[1,16]{1,0:T(1,128)} %bitcast.20, f32[1,16]{1,0:T(1,128)} %bitcast.21, s32[1]{0:T(128)S(6)} %copy.20.lengths, f32[1,2048]{1,0:T(1,128)} %bitcast.18, ...), custom_call_target="tpu_custom_call" | custom-call | tf_op jit(solution)/shard_map/layer/pallas_call | solution.py:704
  31.0 0.6 %copy.19 = bf16[4,2560]{1,0:T(4,128)(2,1)} copy(bf16[4,2560]{1,0:T(4,128)(2,1)S(1)} %layer.1) | data formatting | bytes 40960

commit v4 on v3

--- a/solution.py
+++ b/solution.py
@@ -271,10 +271,10 @@
     out,
     gain, bias, rate, skip, mixer_gain,
     w_a, w_b, k_v, v_v, s_v, g_v, u_v, m_v, d_v,
-    xg, xf, xb, sq_send, sq_recv, p_send, p_recv, c_b, tot, step_f,
+    xg, xf, xb, p_send, p_recv, c_b, tot, step_f,
     f_send, f_recv, feat, bc, qbuf, knbuf, vnbuf, obuf, cbuf, rbuf, own,
-    m_send, m_recv, lhs, gsc, gu_send, gu_recv, hbuf, o_send, o_recv,
-    sem_w, sem_loc, sem_gs, sem_gr, sem_ps, sem_pr, sem_fs, sem_fr,
+    m_send, m_recv, lhs, lhs_b, gsc, gu_send, gu_recv, hbuf, o_send, o_recv,
+    sem_w, sem_loc, sem_r, sem_gs, sem_gr, sem_ps, sem_pr, sem_fs, sem_fr,
     sem_ms, sem_mr, sem_us, sem_ur, sem_hs, sem_hr, sem_os, sem_or,
 ):
     n, n_short, rows, width, gcol, scol, ncol, ocol, fspans, ospans = dims
@@ -289,8 +289,9 @@
     m_heads = MH // n_short
     rep = QUERY_HEADS // KEY_VALUE_HEADS
     acol = gcol + scol + ncol
+    sq_width = round_up(acol + 1) - acol
     fpad = xpad(gcol)
-    opad = round_up(ocol)
+    opad = round_up(ocol + ocol % LANE)
 
     def peer(d):
         return lax.rem(me + d, n)
@@ -310,29 +311,44 @@
         weights.append(copy)
         return copy
 
+    late = n // 2
+    early = me < late
+
+    def tell(sem, wide, short):
+        pl.semaphore_signal(
+            sem, inc=1, device_id={"wide": wide, "short": short}, device_id_type=MESH
+        )
+
     barrier = pltpu.get_barrier_semaphore()
-    for k in range(n):
-        for e in range(n_short):
-            if k < n - 1 or e:
-                pl.semaphore_signal(
-                    barrier, inc=1,
-                    device_id={
-                        "wide": far_first(k) if k < n - 1 else me, "short": lax.rem(s + e, n_short)
-                    },
-                    device_id_type=MESH,
-                )
+    for k in range(late):
+        to = n - 1 - k
+
+        @pl.when(me != to)
+        def _(to=to):
+            tell(barrier, to, s)
+
+    @pl.when(early)
+    def _():
+        for k in range(1, late):
+            tell(barrier, lax.rem(me + k, late), s)
+
+    tell(barrier, me, other)
+
     own_tokens = fetch(tokens, xg.at[me])
     small = [
         fetch(gain_h, gain), fetch(bias_h, bias), fetch(rate_h, rate), fetch(skip_h, skip),
         fetch(mixer_gain_h, mixer_gain),
     ]
     lead = dims_lead(gcol)
-    fa = [
-        fetch(mixer_in.at[s, pl.ds(0, lead)], w_a.at[pl.ds(0, lead)]),
-        fetch(mixer_in.at[other], w_a.at[pl.ds(lead, gcol)]),
-        fetch(shared_in, w_a.at[pl.ds(lead + gcol, scol)]),
-        fetch(step_in, w_a.at[pl.ds(lead + gcol + scol, ncol)]),
-    ]
+    sem_a = len(weights)
+    for src, dst in (
+        (mixer_in.at[s, pl.ds(0, lead)], w_a.at[pl.ds(0, lead)]),
+        (mixer_in.at[other], w_a.at[pl.ds(lead, gcol)]),
+        (shared_in, w_a.at[pl.ds(lead + gcol, scol)]),
+        (step_in, w_a.at[pl.ds(lead + gcol + scol, ncol)]),
+    ):
+        pltpu.make_async_copy(src, dst, sem_w.at[sem_a]).start()
+    weights.append(None)
     fb = [fetch(mixer_in.at[s, pl.ds(lead, gcol - lead)], w_b)]
 
     def cols(c):
@@ -346,10 +362,11 @@
         if c == 0:
             fkv = [fetch(keys, k_v), fetch(values, v_v), fetch(state, s_v)]
     fdn = [fetch(down.at[cols(c)], d_v.at[cols(c)]) for c in range(n_chunk)]
-    fmo = [fetch(mixer_out.at[g], m_v.at[g, pl.ds(0, ocol)]) for g in range(n_short)]
-
-    own_tokens.wait()
-    pl.semaphore_wait(barrier, n * n_short - 1)
+    sem_m = len(weights)
+    for g in range(n_short):
+        pltpu.make_async_copy(
+            mixer_out.at[g], m_v.at[pl.ds(g * ocol, ocol)], sem_w.at[sem_m]
+        ).start()
 
     def remote(src, dst, send, recv, wide, short):
         copy = pltpu.make_async_remote_copy(
@@ -364,11 +381,27 @@
 
     sent = []
 
-    for k in range(n - 1):
-        remote(xg.at[me], xg.at[me], sem_gs, sem_gr, far_first(k), s)
-    for g in range(n_short):
-        if opad > ocol:
-            m_v[g, ocol:opad, :] = jnp.zeros((opad - ocol, width), BF16)
+    def give(wide):
+        remote(tokens, xg.at[me], sem_gs, sem_gr, wide, s)
+
+    pl.semaphore_wait(barrier, jnp.where(early, late, n))
+
+    @pl.when(early)
+    def _():
+        for k in range(1, late):
+            give(lax.rem(me + k, late))
+        pl.semaphore_wait(sem_r, 1)
+        for k in range(late):
+            give(n - 1 - k)
+
+    @pl.when(me >= late)
+    def _():
+        tell(sem_r, jnp.where(me >= n - 2, me - (n - 2), me - 2), s)
+        for k in range(late):
+            give(k)
+        for k in range(1, late):
+            give(late + lax.rem(me + k, late))
+
     feat[...] = jnp.zeros_like(feat)
     bc[...] = jnp.zeros_like(bc)
     qbuf[...] = jnp.zeros_like(qbuf)
@@ -381,31 +414,30 @@
     for copy in small:
         copy.wait()
     cos_t, sin_t = rope_rows(lengths[0], rows)
+    own_tokens.wait()
     arrived(xg.at[pl.ds(0, n - 1)], sem_gr)
     for j in range(n):
         xf[rows * j : rows * (j + 1), :] = xg[j].astype(F32)
     x = xf[...]
-    sq_send[...] = jnp.broadcast_to(jnp.sum(x * x, axis=1, keepdims=True), sq_send.shape)
-    sent.append(remote(sq_send, sq_recv, sem_ps.at[0], sem_pr.at[0], me, other))
+    squares = jnp.sum(x * x, axis=1, keepdims=True)
+    p_send[:, acol:] = jnp.broadcast_to(squares, (total_rows, sq_width))
     for j in range(width // LANE):
         lanes = slice(j * LANE, (j + 1) * LANE)
         xb[:, lanes] = (xf[:, lanes] * gain[j : j + 1, :]).astype(BF16)
 
-    for copy in fa:
-        copy.wait()
+    arrived(w_a, sem_w.at[sem_a])
     both = dot_nt(xb[...], w_a[...])
-    p_send[...] = both[:, lead:]
+    p_send[:, :acol] = both[:, lead:]
     c_b[:, :lead] = both[:, :lead]
-    sent.append(remote(p_send, p_recv, sem_ps.at[1], sem_pr.at[1], me, other))
+    sent.append(remote(p_send, p_recv, sem_ps, sem_pr, me, other))
     fb[0].wait()
     c_b[:, lead:gcol] = dot_nt(xb[...], w_b[...])
     lane = lax.broadcasted_iota(jnp.int32, (total_rows, acol), 1)
-    mine = jnp.where(lane < gcol, c_b[:, :acol], p_send[...])
-    arrived(sq_recv, sem_pr.at[0])
-    mean_square = (sq_send[:, :1] + sq_recv[:, :1]) / D
+    mine = jnp.where(lane < gcol, c_b[:, :acol], p_send[:, :acol])
+    arrived(p_recv, sem_pr)
+    mean_square = (squares + p_recv[:, acol : acol + 1]) / D
     inv = lax.rsqrt(mean_square + epsilon)
-    arrived(p_recv, sem_pr.at[1])
-    tot[:, :acol] = (mine + p_recv[...]) * inv
+    tot[:, :acol] = (mine + p_recv[:, :acol]) * inv
     whole = tot[...]
     wide_lane = lax.broadcasted_iota(jnp.int32, whole.shape, 1)
     span = whole.shape[1]
@@ -433,9 +465,8 @@
     def gate_up(c):
         part = slice(fspans[c][0], fspans[c][0] + fspans[c][1])
         fgu[c][0].wait()
-        both = [dot(xb[...], g_v[:, part])]
         fgu[c][1].wait()
-        both.append(dot(xb[...], u_v[:, part]))
+        both = [dot(xb[...], g_v[:, part]), dot(xb[...], u_v[:, part])]
         for k in range(2):
             for i in range(n_short):
                 gsc[k, i, :, part] = both[k][half * i : half * (i + 1)] * inv[half * i : half * (i + 1)]
@@ -459,18 +490,16 @@
             )
         )
 
-    def down_part(c):
-        part = slice(fspans[c][0], fspans[c][0] + fspans[c][1])
+    def down_part(at, size):
+        part = slice(at, at + size)
+        term = dot(hbuf[:, :, part].reshape(total_rows, size), d_v[part, :])
+        xf[...] = term if at == 0 else xf[...] + term
+
+    def hidden_in(c):
         arrived(hbuf.at[other, :, cols(c)], sem_hr.at[c])
         fdn[c].wait()
-        term = dot(hbuf[:, :, part].reshape(total_rows, fspans[c][1]), d_v[part, :])
-        xf[...] = term if c == 0 else xf[...] + term
-
-    early = max(1, n_chunk - 1)
-    for c in range(early):
-        gate_up(c)
-        if c:
-            hidden(c - 1)
+
+    gate_up(0)
 
     own_f.wait()
     arrived(f_recv.at[pl.ds(0, n - 1)], sem_fr)
@@ -573,20 +602,34 @@
     own_m = pltpu.make_async_copy(m_send.at[me], m_recv.at[s * n + me], sem_loc.at[1])
     own_m.start()
 
-    for c in range(early, n_chunk):
+    hidden(0)
+    for c in range(1, n_chunk):
         gate_up(c)
-        hidden(c - 1)
-    for c in range(n_chunk):
-        if c == max(0, n_chunk - 2):
-            hidden(n_chunk - 1)
-        down_part(c)
+    hidden_in(0)
+    pieces = spans_of(fspans[0][1], 1024)
+    for k, (at, size) in enumerate(pieces):
+        if k == len(pieces) - 1:
+            for c in range(1, n_chunk):
+                hidden(c)
+        down_part(at, size)
+    for c in range(1, n_chunk):
+        hidden_in(c)
+        down_part(*fspans[c])
     own_m.wait()
     arrived(m_recv.at[pl.ds(0, n * n_short - 1)], sem_mr)
     for g in range(n_short):
         for j in range(n):
             lhs[g, rows * j : rows * (j + 1), :] = m_recv[g * n + j].astype(F32)
-    for copy in fmo:
-        copy.wait()
+    shift = ocol % LANE
+    at = ocol - shift
+    block_lane = lax.broadcasted_iota(jnp.int32, (total_rows, opad), 1)
+    first = jnp.where(block_lane < ocol, lhs[0], 0.0)
+    second = pltpu.roll(lhs[1], shift, 1) if shift else lhs[1]
+    second = jnp.where((block_lane >= shift) & (block_lane < shift + ocol), second, 0.0)
+    lhs_b[:, :at] = first[:, :at].astype(BF16)
+    lhs_b[:, at:opad] = (first[:, at:] + second[:, : opad - at]).astype(BF16)
+    lhs_b[:, opad:] = second[:, opad - at :].astype(BF16)
+    arrived(m_v, sem_w.at[sem_m])
     def out_to(o, k):
         to = upward(k)
         part = pl.ds(*ospans[o])
@@ -594,9 +637,7 @@
 
     for o in range(n_oc):
         oc = slice(ospans[o][0], ospans[o][0] + ospans[o][1])
-        acc = xf[:, oc]
-        for g in range(n_short):
-            acc = acc + dot(lhs[g].astype(BF16), m_v[g, :, oc])
+        acc = xf[:, oc] + dot(lhs_b[:, : n_short * ocol], m_v[:, oc])
         xf[:, oc] = acc
         for r in range(n):
             o_send[r, :, oc] = xf[rows * r : rows * (r + 1), oc].astype(BF16)
@@ -651,17 +692,18 @@
     ncol = step_in.shape[1]
     ocol = mixer_out.shape[1]
     ffl = gate_weight.shape[1]
-    fspans = spans_of(ffl, 1024)
-    first = min(512, width)
-    ospans = ((0, first),) + tuple((first + at, size) for at, size in spans_of(width - first, 1024))
+    fspans = spans_of(ffl, 2048)
+    first = min(1024, width)
+    ospans = ((0, first),) + tuple((first + at, size) for at, size in spans_of(width - first, 1536))
     n_chunk = len(fspans)
     n_oc = len(ospans)
     m_heads = MH // n_short
     kv_heads = KEY_VALUE_HEADS // n_short
     total_rows = n * rows
     acol = gcol + scol + ncol
+    sq_width = round_up(acol + 1) - acol
     fpad = xpad(gcol)
-    opad = round_up(ocol)
+    opad = round_up(ocol + ocol % LANE)
     lead = dims_lead(gcol)
     features = n * gcol
     outs = n * ocol
@@ -679,10 +721,10 @@
         V((lead + acol, width), BF16), V((gcol - lead, width), BF16), V((slots, kvw), BF16),
         V((slots, kvw), BF16), V((m_heads * MP, NS), BF16),
         V((width, ffl), BF16), V((width, ffl), BF16),
-        V((n_short, opad, width), BF16), V((ffl, width), BF16),
+        V((n_short * ocol, width), BF16), V((ffl, width), BF16),
         V((n, rows, width), BF16), V((total_rows, width), F32), V((total_rows, width), BF16),
-        V((total_rows, LANE), F32), V((total_rows, LANE), F32),
-        V((total_rows, acol), F32), V((total_rows, acol), F32), V((total_rows, fpad), F32),
+        V((total_rows, acol + sq_width), F32), V((total_rows, acol + sq_width), F32),
+        V((total_rows, fpad), F32),
         V((total_rows, fpad), F32), V((total_rows, LANE), F32),
         V((n, rows, fpad + LANE), BF16), V((n, rows, fpad + LANE), BF16),
         V((rows, features), F32), V((rows, 2 * NS), F32),
@@ -691,13 +733,13 @@
         V((16, NS), F32), V((16, m_heads * MP), F32),
         V((rows, round_up(outs) + opad + LANE), F32),
         V((n, rows, opad), BF16), V((n_short * n, rows, opad), BF16),
-        V((n_short, total_rows, opad), F32),
+        V((n_short, total_rows, opad), F32), V((total_rows, ocol // LANE * LANE + opad), BF16),
         V((2, n_short, half, ffl), F32),
         V((2, half, ffl), BF16), V((2, half, ffl), BF16),
         V((n_short, half, ffl), BF16),
         V((n, rows, width), BF16), V((n, rows, width), BF16),
-        dma((6 + 5 + 3 * n_chunk + 3 + n_short,)), dma((2,)),
-        dma, dma, dma((2,)), dma((2,)), dma, dma,
+        dma((6 + 2 + 3 * n_chunk + 3 + 1,)), dma((2,)),
+        pltpu.SemaphoreType.REGULAR, dma, dma, dma, dma, dma, dma,
         dma, dma, dma((n_chunk,)), dma((n_chunk,)),
         dma((n_chunk,)), dma((n_chunk,)), dma((n_oc,)), dma((n_oc,)),
     ]
@@ -731,6 +773,7 @@
         and LANE % shared_in.shape[1] == 0
         and step_in.shape[1] % 16 == 0
         and args[13].shape[1] % 16 == 0
+        and args[13].shape[1] >= LANE
         and args[14].shape[1] % LANE == 0
         and tokens.shape[1] % LANE == 0
     )

time: 31.8 us -> 30.7 us (0.965)
  Pallas kernels: 30.4 us -> 29.3 us
    pallas_call x1, Pallas kernels: 30.4 us -> 29.3 us  [fused(): pl.pallas_call(functools.partial(fused_kernel, dims), out_shape=pltpu.VME...]
where the time goes in v4:
time: 30.7 us; the launch traced here: 30.6 us
  Pallas kernels  29.3 us (95%)
  between operations  0.66 us (2%)
  local copies, waits for them, and re-layouts  0.61 us (2%)
    pallas_call x1, Pallas kernels, fused(): pl.pallas_call(functools.partial(fused_kernel, dims), out_shape=pltpu.VME...  29.3 us

profile of v4, /device:TPU:0, one launch (start us, length us, event | category | flops | bytes accessed | tf_op | source)
XLA Modules:
  0.0 30.6 jit_solution(14141859175205894453)
XLA Ops:
  0.7 29.3 %layer.1 = bf16[4,2560]{1,0:T(4,128)(2,1)S(1)} custom-call(bf16[4,2560]{1,0:T(4,128)(2,1)} %tokens.1, f32[20,128]{1,0:T(8,128)} %bitcast.17, f32[1,16]{1,0:T(1,128)} %bitcast.19, f32[1,16]{1,0:T(1,128)} %bitcast.20, f32[1,16]{1,0:T(1,128)} %bitcast.21, s32[1]{0:T(128)S(6)} %copy.20.lengths, f32[1,2048]{1,0:T(1,128)} %bitcast.18, ...), custom_call_target="tpu_custom_call" | custom-call | tf_op jit(solution)/shard_map/layer/pallas_call | solution.py:746
  30.0 0.6 %copy.19 = bf16[4,2560]{1,0:T(4,128)(2,1)} copy(bf16[4,2560]{1,0:T(4,128)(2,1)S(1)} %layer.1) | data formatting | bytes 40960

commit v5 on v4

--- a/solution.py
+++ b/solution.py
@@ -273,7 +273,7 @@
     w_a, w_b, k_v, v_v, s_v, g_v, u_v, m_v, d_v,
     xg, xf, xb, p_send, p_recv, c_b, tot, step_f,
     f_send, f_recv, feat, bc, qbuf, knbuf, vnbuf, obuf, cbuf, rbuf, own,
-    m_send, m_recv, lhs, lhs_b, gsc, gu_send, gu_recv, hbuf, o_send, o_recv,
+    m_send, m_recv, lhs, lhs_b, gsc, gu_send, gu_recv, gl_send, gl_recv, hbuf, o_send, o_recv,
     sem_w, sem_loc, sem_r, sem_gs, sem_gr, sem_ps, sem_pr, sem_fs, sem_fr,
     sem_ms, sem_mr, sem_us, sem_ur, sem_hs, sem_hr, sem_os, sem_or,
 ):
@@ -323,7 +323,7 @@
     for k in range(late):
         to = n - 1 - k
 
-        @pl.when(me != to)
+        @pl.when((me != to) if to >= n - 2 else (me != to) & (me != 2 * n - 5 - to))
         def _(to=to):
             tell(barrier, to, s)
 
@@ -382,25 +382,43 @@
     sent = []
 
     def give(wide):
-        remote(tokens, xg.at[me], sem_gs, sem_gr, wide, s)
-
-    pl.semaphore_wait(barrier, jnp.where(early, late, n))
+        remote(xg.at[me], xg.at[me], sem_gs, sem_gr, wide, s)
+
+    pl.semaphore_wait(barrier, jnp.where(early, late, jnp.where(me < n - 2, n - 1, n)))
+    own_tokens.wait()
+    side = lax.rem(me, 2)
+    beside = me + 1 - 2 * side
 
     @pl.when(early)
     def _():
         for k in range(1, late):
             give(lax.rem(me + k, late))
-        pl.semaphore_wait(sem_r, 1)
-        for k in range(late):
-            give(n - 1 - k)
-
-    @pl.when(me >= late)
+        pl.semaphore_wait(sem_r.at[0], 1)
+        give(n - 2 + side)
+        give(n - 3 - side)
+        give(n - 4 + side)
+        pl.semaphore_wait(sem_r.at[1], 1)
+        give(n - 1 - side)
+
+    @pl.when((me >= late) & (me < n - 2))
     def _():
-        tell(sem_r, jnp.where(me >= n - 2, me - (n - 2), me - 2), s)
+        tell(sem_r.at[0], me - 2, s)
+        tell(sem_r.at[0], me - 4, s)
+        tell(sem_r.at[1], beside - 2, s)
+        tell(sem_r.at[1], beside - 4, s)
+        tell(sem_r.at[0], beside, s)
         for k in range(late):
             give(k)
-        for k in range(1, late):
-            give(late + lax.rem(me + k, late))
+        give(beside)
+        give(n - 2 + side)
+        pl.semaphore_wait(sem_r.at[0], 1)
+        give(n - 1 - side)
+
+    @pl.when(me >= n - 2)
+    def _():
+        for k in range(n - 2):
+            give(k)
+        give(beside)
 
     feat[...] = jnp.zeros_like(feat)
     bc[...] = jnp.zeros_like(bc)
@@ -414,7 +432,6 @@
     for copy in small:
         copy.wait()
     cos_t, sin_t = rope_rows(lengths[0], rows)
-    own_tokens.wait()
     arrived(xg.at[pl.ds(0, n - 1)], sem_gr)
     for j in range(n):
         xf[rows * j : rows * (j + 1), :] = xg[j].astype(F32)
@@ -444,16 +461,12 @@
     features = pltpu.roll(
         jnp.where(wide_lane < gcol, whole, 0.0), lax.rem(me * gcol, LANE), 1
     )
-    low = pltpu.roll(whole, span - gcol, 1)[:, :LANE]
-    low_lane = lax.broadcasted_iota(jnp.int32, low.shape, 1)
-    low = pltpu.roll(jnp.where(low_lane < scol, low, 0.0), lax.rem(me * scol, LANE), 1)
+    low = pltpu.roll(whole, span - scol - gcol, 1)
     step_all = pltpu.roll(whole, span - gcol - scol, 1)[:, :LANE]
     step_f[...] = pltpu.roll(step_all, lax.rem(LANE - s * m_heads, LANE), 1)
-    tot[...] = features
-    c_b[:, :LANE] = low
+    tot[...] = jnp.where(wide_lane < span - scol, features, low)
     for r in range(n):
-        f_send[r, :, :fpad] = tot[rows * r : rows * (r + 1), :].astype(BF16)
-        f_send[r, :, fpad:] = c_b[rows * r : rows * (r + 1), :LANE].astype(BF16)
+        f_send[r] = tot[rows * r : rows * (r + 1), :].astype(BF16)
     for k in range(n - 1):
         to = far_first(k)
         remote(f_send.at[to], f_recv.at[me], sem_fs, sem_fr, to, s)
@@ -470,6 +483,17 @@
         for k in range(2):
             for i in range(n_short):
                 gsc[k, i, :, part] = both[k][half * i : half * (i + 1)] * inv[half * i : half * (i + 1)]
+        if c:
+            late_cols = pl.ds(fspans[c][0] - fspans[0][1], fspans[c][1])
+            for k in range(2):
+                gl_send[k, :, late_cols] = (both[k] * inv).astype(BF16)
+            sent.append(
+                remote(
+                    gl_send.at[:, :, late_cols], gl_recv.at[:, :, late_cols],
+                    sem_us.at[c], sem_ur.at[c], me, other,
+                )
+            )
+            return
         for k in range(2):
             gu_send[k, :, part] = gsc[k, other, :, part].astype(BF16)
         sent.append(
@@ -480,6 +504,15 @@
 
     def hidden(c):
         part = slice(fspans[c][0], fspans[c][0] + fspans[c][1])
+        if c:
+            late_cols = pl.ds(fspans[c][0] - fspans[0][1], fspans[c][1])
+            arrived(gl_recv.at[:, :, late_cols], sem_ur.at[c])
+            for i in range(n_short):
+                here = slice(half * i, half * (i + 1))
+                a = gsc[0, i, :, part] + gl_recv[0, here, late_cols].astype(F32)
+                b = gsc[1, i, :, part] + gl_recv[1, here, late_cols].astype(F32)
+                hbuf[i, :, part] = (silu(a) * b).astype(BF16)
+            return
         arrived(gu_recv.at[:, :, cols(c)], sem_ur.at[c])
         a = gsc[0, s, :, part] + gu_recv[0, :, part].astype(F32)
         b = gsc[1, s, :, part] + gu_recv[1, :, part].astype(F32)
@@ -496,7 +529,8 @@
         xf[...] = term if at == 0 else xf[...] + term
 
     def hidden_in(c):
-        arrived(hbuf.at[other, :, cols(c)], sem_hr.at[c])
+        if c == 0:
+            arrived(hbuf.at[other, :, cols(c)], sem_hr.at[c])
         fdn[c].wait()
 
     gate_up(0)
@@ -504,12 +538,20 @@
     own_f.wait()
     arrived(f_recv.at[pl.ds(0, n - 1)], sem_fr)
     fwidth = feat.shape[1]
+    tail_lane = lax.broadcasted_iota(jnp.int32, (rows, LANE), 1)
     for j in range(n):
         base = gcol * j // LANE * LANE
         w = min(fpad, fwidth - base)
-        feat[:, base : base + w] += f_recv[j, :, :w].astype(F32)
+        block = f_recv[j].astype(F32)
+        tail = block[:, fpad - LANE :]
+        block = jnp.concatenate(
+            [block[:, : fpad - LANE], jnp.where(tail_lane < LANE - scol, tail, 0.0)], axis=1
+        )
+        feat[:, base : base + w] += block[:, :w]
         base = scol * j // LANE * LANE
-        bc[:, base : base + LANE] += f_recv[j, :, fpad:].astype(F32)
+        tail = jnp.where(tail_lane < LANE - scol, 0.0, tail)
+        move = (scol * (j + 1)) % LANE
+        bc[:, base : base + LANE] += pltpu.roll(tail, move, 1) if move else tail
     for copy in fkv:
         copy.wait()
     k_at = q_heads * HEAD_SIZE
@@ -699,6 +741,7 @@
     n_oc = len(ospans)
     m_heads = MH // n_short
     kv_heads = KEY_VALUE_HEADS // n_short
+    remain = max(LANE, ffl - fspans[0][1])
     total_rows = n * rows
     acol = gcol + scol + ncol
     sq_width = round_up(acol + 1) - acol
@@ -726,7 +769,7 @@
         V((total_rows, acol + sq_width), F32), V((total_rows, acol + sq_width), F32),
         V((total_rows, fpad), F32),
         V((total_rows, fpad), F32), V((total_rows, LANE), F32),
-        V((n, rows, fpad + LANE), BF16), V((n, rows, fpad + LANE), BF16),
+        V((n, rows, fpad), BF16), V((n, rows, fpad), BF16),
         V((rows, features), F32), V((rows, 2 * NS), F32),
         V((kv_heads, 32, HEAD_SIZE), F32), V((kv_heads, 16, HEAD_SIZE), F32),
         V((kv_heads, 16, HEAD_SIZE), F32), V((kv_heads, 32, HEAD_SIZE), F32),
@@ -736,12 +779,13 @@
         V((n_short, total_rows, opad), F32), V((total_rows, ocol // LANE * LANE + opad), BF16),
         V((2, n_short, half, ffl), F32),
         V((2, half, ffl), BF16), V((2, half, ffl), BF16),
+        V((2, total_rows, remain), BF16), V((2, total_rows, remain), BF16),
         V((n_short, half, ffl), BF16),
         V((n, rows, width), BF16), V((n, rows, width), BF16),
         dma((6 + 2 + 3 * n_chunk + 3 + 1,)), dma((2,)),
-        pltpu.SemaphoreType.REGULAR, dma, dma, dma, dma, dma, dma,
+        pltpu.SemaphoreType.REGULAR((2,)), dma, dma, dma, dma, dma, dma,
         dma, dma, dma((n_chunk,)), dma((n_chunk,)),
-        dma((n_chunk,)), dma((n_chunk,)), dma((n_oc,)), dma((n_oc,)),
+        dma((1,)), dma((1,)), dma((n_oc,)), dma((n_oc,)),
     ]
     return pl.pallas_call(
         functools.partial(fused_kernel, dims),
@@ -762,6 +806,10 @@
     )
 
 
+def roomy(n, gcol, scol):
+    return max(gcol * j % LANE for j in range(n)) + gcol <= xpad(gcol) - scol
+
+
 def fits(n, n_short, args):
     tokens, mixer_in, shared_in, step_in = args[0], args[2], args[3], args[4]
     return (
@@ -771,6 +819,8 @@
         and mixer_in.shape[2] % 16 == 0
         and shared_in.shape[1] % 16 == 0
         and LANE % shared_in.shape[1] == 0
+        and shared_in.shape[1] < LANE
+        and roomy(n, mixer_in.shape[2], shared_in.shape[1])
         and step_in.shape[1] % 16 == 0
         and args[13].shape[1] % 16 == 0
         and args[13].shape[1] >= LANE

time: 30.7 us -> 30.5 us (level)
  no operation moved by 1% of the time
where the time goes in v5:
time: 30.5 us; the launch traced here: 30.3 us
  Pallas kernels  29 us (95%)
  between operations  0.66 us (2%)
  local copies, waits for them, and re-layouts  0.61 us (2%)
    pallas_call x1, Pallas kernels, fused(): pl.pallas_call(functools.partial(fused_kernel, dims), out_shape=pltpu.VME...  29 us

profile of v5, /device:TPU:0, one launch (start us, length us, event | category | flops | bytes accessed | tf_op | source)
XLA Modules:
  0.0 30.3 jit_solution(15488846215273286892)
XLA Ops:
  0.7 29.0 %layer.1 = bf16[4,2560]{1,0:T(4,128)(2,1)S(1)} custom-call(bf16[4,2560]{1,0:T(4,128)(2,1)} %tokens.1, f32[20,128]{1,0:T(8,128)} %bitcast.17, f32[1,16]{1,0:T(1,128)} %bitcast.19, f32[1,16]{1,0:T(1,128)} %bitcast.20, f32[1,16]{1,0:T(1,128)} %bitcast.21, s32[1]{0:T(128)S(6)} %copy.20.lengths, f32[1,2048]{1,0:T(1,128)} %bitcast.18, ...), custom_call_target="tpu_custom_call" | custom-call | tf_op jit(solution)/shard_map/layer/pallas_call | solution.py:790
  29.7 0.6 %copy.19 = bf16[4,2560]{1,0:T(4,128)(2,1)} copy(bf16[4,2560]{1,0:T(4,128)(2,1)S(1)} %layer.1) | data formatting | bytes 40960
